TPU v7x, 32 devices: a whole 2x2x4 slice. The times are simulated.
32 devices in a mesh: fsdp: 4 (over y, core), ctx: 2 (over x), tp: 4 (over z).
Axes of the slice: x: 2, y: 2, z: 4, core: 2. Of those that a mesh axis runs over, the one named last changes fastest.
Arguments:
- inputs: bfloat16 [2, 8, 512, 1024], P(None, 'fsdp', 'ctx'), may hold values from -6 to 6
- out_grad: bfloat16 [2, 8, 512, 1024], P(None, 'fsdp', 'ctx'), may hold values from -6 to 6
- segment_ids: int32 [2, 8, 512], P(None, 'fsdp'), may hold values from 0 to 7, never falling along the last dimension, each value on 1 to 256 neighbouring positions
- w_qkv: bfloat16 [1024, 3072], P(('fsdp', 'ctx'), 'tp'), may hold values from -0.25 to 0.25
- bias_qv: bfloat16 [2048], P('tp'), may hold values from -3 to 3
- w_out: bfloat16 [1024, 1024], P(('fsdp', 'ctx'), 'tp'), may hold values from -0.25 to 0.25
- w_up: bfloat16 [1024, 4096], P(('fsdp', 'ctx'), 'tp'), may hold values from -0.1875 to 0.1875
- bias_up: bfloat16 [4096], P('tp'), may hold values from -2 to 2
- w_down: bfloat16 [1024, 4096], P(('fsdp', 'ctx'), 'tp'), may hold values from -0.125 to 0.125
- gains: bfloat16 [1024, 2], P(('fsdp', 'ctx')), may hold values from 0.25 to 1.75
- shifts: bfloat16 [1024, 4], P(('fsdp', 'ctx')), may hold values from -2 to 2
Outputs:
- layer_out: bfloat16 [2, 8, 512, 1024], P(None, 'fsdp', ('ctx', 'tp'))
- input_grad: float32 [2, 8, 512, 1024], P(None, 'fsdp', ('ctx', 'tp'))
- grad_w_qkv: float32 [1024, 3072], P(('fsdp', 'ctx'), 'tp')
- grad_bias_qv: float32 [2048], P('tp')
- grad_w_out: float32 [1024, 1024], P(('fsdp', 'ctx'), 'tp')
- grad_w_up: float32 [1024, 4096], P(('fsdp', 'ctx'), 'tp')
- grad_bias_up: float32 [4096], P('tp')
- grad_w_down: float32 [1024, 4096], P(('fsdp', 'ctx'), 'tp')
- grad_gains: float32 [1024, 2], P(('fsdp', 'ctx'))
- grad_shifts: float32 [1024, 4], P(('fsdp', 'ctx'))
Inputs may be any that keep to these rules, and one draw needn't show every extreme that they name: `segment_ids`: within a sequence the ids never fall; each of the 8 documents holds 1 to 256 positions, and one holds exactly 256.
All inputs are finite; a program needn't handle non-finite values.
Results may differ from a plain program's by a relative error of at most 0.018.
Values may be sent and summed in bfloat16 or wider, within the bound.
A program may use at most 64 MiB of HBM per device.

v0:
```python
import jax
import jax.numpy as jnp
from jax import lax
from jax.sharding import PartitionSpec as P

HD = 64


norm_epsilon = 1e-12
masked_score = -1e30


def norm_rows(rows_in, gain_row, offset):
    average = jnp.mean(rows_in, axis=-1, keepdims=True)
    centered = rows_in - average
    spread = jnp.mean(centered * centered, axis=-1, keepdims=True)
    return centered * lax.rsqrt(spread + norm_epsilon) * gain_row + offset


def exact_gelu(rows_in):
    return jax.nn.gelu(rows_in, approximate=False)


def contract_rows(left_rows, right_rows):
    return lax.dot_general(
        left_rows, right_rows, (((0,), (0,)), ((), ())), preferred_element_type=jnp.float32
    )


def times_transposed(left_rows, right_rows):
    return lax.dot_general(
        left_rows, right_rows, (((1,), (1,)), ((), ())), preferred_element_type=jnp.float32
    )


def masked_scores(queries, key_rows, same_segment, score_scale):
    scores = (
        jnp.einsum("sqhe,skhe->shqk", queries, key_rows, preferred_element_type=jnp.float32)
        * score_scale
    )
    return jnp.where(same_segment[:, None], scores, masked_score)


def add_pair(running, update):
    return running + update


def reduce_rows(part):
    return lax.psum(part, "tp")


def local(
    inputs, out_grad, segment_ids, w_qkv, bias_qv, w_out, w_up, bias_up, w_down, gains, shifts
):
    batches, seq_local, rows_local, model_width = inputs.shape
    tokens = seq_local * rows_local
    heads_local = w_out.shape[1] // HD
    score_scale = HD ** (-0.5)
    row_share = rows_local // lax.axis_size("tp")
    row_start = lax.axis_index("tp") * row_share
    query_start = lax.axis_index("ctx") * rows_local
    qv_bias = bias_qv.astype(jnp.float32).reshape(heads_local, 2, HD)
    up_bias = bias_up.astype(jnp.float32)

    def pick_rows(values):
        shaped = values.reshape(seq_local, rows_local, model_width)
        return lax.dynamic_slice_in_dim(shaped, row_start, row_share, 1)

    full_totals = (
        jnp.zeros((model_width, w_qkv.shape[1]), jnp.float32),
        jnp.zeros((model_width, w_out.shape[1]), jnp.float32),
        jnp.zeros((model_width, w_up.shape[1]), jnp.float32),
        jnp.zeros((model_width, w_down.shape[1]), jnp.float32),
        jnp.zeros((model_width, 2), jnp.float32),
        jnp.zeros((model_width, 4), jnp.float32),
    )
    share_totals = (
        jnp.zeros(w_qkv.shape, jnp.float32),
        jnp.zeros(w_out.shape, jnp.float32),
        jnp.zeros(w_up.shape, jnp.float32),
        jnp.zeros(w_down.shape, jnp.float32),
        jnp.zeros(gains.shape, jnp.float32),
        jnp.zeros(shifts.shape, jnp.float32),
    )
    qv_bias_grad = jnp.zeros(bias_qv.shape, jnp.float32)
    up_bias_grad = jnp.zeros(bias_up.shape, jnp.float32)
    layer_rows = []
    input_rows = []
    for batch_index in range(batches):
        gathered = (
            lax.all_gather(w_qkv, ("fsdp", "ctx"), axis=0, tiled=True),
            lax.all_gather(w_out, ("fsdp", "ctx"), axis=0, tiled=True),
            lax.all_gather(w_up, ("fsdp", "ctx"), axis=0, tiled=True),
            lax.all_gather(w_down, ("fsdp", "ctx"), axis=0, tiled=True),
            lax.all_gather(gains, ("fsdp", "ctx"), axis=0, tiled=True),
            lax.all_gather(shifts, ("fsdp", "ctx"), axis=0, tiled=True),
        )
        full_qkv, full_out, full_up, full_down, full_gains, full_shifts = gathered
        gain_rows = full_gains.astype(jnp.float32)
        shift_rows = full_shifts.astype(jnp.float32)
        x_low = inputs[batch_index].reshape(tokens, model_width)
        x_full = x_low.astype(jnp.float32)
        projected = jnp.dot(x_low, full_qkv, preferred_element_type=jnp.float32)
        projected = projected.reshape(seq_local, rows_local, heads_local, 3, HD)
        queries = (projected[:, :, :, 0] + qv_bias[:, 0]).astype(jnp.bfloat16)
        key_local = projected[:, :, :, 1].astype(jnp.bfloat16)
        value_local = (projected[:, :, :, 2] + qv_bias[:, 1]).astype(jnp.bfloat16)
        joined = jnp.concatenate([key_local, value_local], axis=-1)
        joined_all = lax.all_gather(joined, "ctx", axis=1, tiled=True)
        key_rows = joined_all[..., :HD]
        value_rows = joined_all[..., HD:]
        segments = segment_ids[batch_index]
        query_segments = lax.dynamic_slice_in_dim(segments, query_start, rows_local, 1)
        same_segment = query_segments[:, :, None] == segments[:, None, :]
        scores = masked_scores(queries, key_rows, same_segment, score_scale)
        row_max = jnp.max(scores, axis=-1, keepdims=True)
        weights = jnp.exp(scores - row_max)
        row_total = jnp.sum(weights, axis=-1, keepdims=True)
        log_total = row_max + jnp.log(row_total)
        p_low = (weights / row_total).astype(jnp.bfloat16)
        attended = jnp.einsum(
            "shqk,skhe->sqhe", p_low, value_rows, preferred_element_type=jnp.float32
        )
        attended_low = attended.reshape(tokens, heads_local * HD).astype(jnp.bfloat16)
        attention_part = times_transposed(attended_low, full_out)
        upstream_full = out_grad[batch_index].reshape(tokens, model_width).astype(jnp.float32)
        attention_total = reduce_rows(attention_part)
        first_sum = x_full + attention_total + shift_rows[:, 0]
        first_norm, first_back = jax.vjp(norm_rows, first_sum, gain_rows[:, 0], shift_rows[:, 1])
        norm_low = first_norm.astype(jnp.bfloat16)
        before_act = jnp.dot(norm_low, full_up, preferred_element_type=jnp.float32) + up_bias
        activated, gelu_back = jax.vjp(exact_gelu, before_act)
        hidden = activated.astype(jnp.bfloat16)
        down_part = times_transposed(hidden, full_down)
        down_total = reduce_rows(down_part)
        second_sum = first_norm + down_total + shift_rows[:, 2]
        result, second_back = jax.vjp(norm_rows, second_sum, gain_rows[:, 1], shift_rows[:, 3])
        layer_rows.append(pick_rows(result).astype(jnp.bfloat16))
        second_grad, gain_two, shift_three = second_back(upstream_full)
        shift_two = jnp.sum(second_grad, axis=0)
        second_low = second_grad.astype(jnp.bfloat16)
        down_step = contract_rows(second_low, hidden)
        hidden_grad = jnp.dot(second_low, full_down, preferred_element_type=jnp.float32)
        (act_grad,) = gelu_back(hidden_grad)
        up_bias_grad = up_bias_grad + jnp.sum(act_grad, axis=0)
        act_low = act_grad.astype(jnp.bfloat16)
        up_step = contract_rows(norm_low, act_low)
        back_part = times_transposed(act_low, full_up)
        back_total = reduce_rows(back_part)
        norm_grad = second_grad + back_total
        first_grad, gain_one, shift_one = first_back(norm_grad)
        shift_zero = jnp.sum(first_grad, axis=0)
        first_low = first_grad.astype(jnp.bfloat16)
        out_step = contract_rows(first_low, attended_low)
        attended_grad = jnp.dot(first_low, full_out, preferred_element_type=jnp.float32)
        attended_grad = attended_grad.astype(jnp.bfloat16).reshape(
            seq_local, rows_local, heads_local, HD
        )
        scores = masked_scores(queries, key_rows, same_segment, score_scale)
        probabilities = jnp.exp(scores - log_total)
        value_grad = jnp.einsum(
            "shqk,sqhe->skhe",
            probabilities.astype(jnp.bfloat16),
            attended_grad,
            preferred_element_type=jnp.float32,
        )
        prob_grad = jnp.einsum(
            "sqhe,skhe->shqk", attended_grad, value_rows, preferred_element_type=jnp.float32
        )
        row_dot = jnp.sum(prob_grad * probabilities, axis=-1, keepdims=True)
        score_grad = (probabilities * (prob_grad - row_dot)).astype(jnp.bfloat16)
        query_grad = (
            jnp.einsum("shqk,skhe->sqhe", score_grad, key_rows, preferred_element_type=jnp.float32)
            * score_scale
        )
        key_grad = (
            jnp.einsum("shqk,sqhe->skhe", score_grad, queries, preferred_element_type=jnp.float32)
            * score_scale
        )
        kv_grads = lax.psum_scatter(
            jnp.concatenate([key_grad, value_grad], axis=-1).astype(jnp.bfloat16),
            "ctx",
            scatter_dimension=1,
            tiled=True,
        ).astype(jnp.float32)
        key_mine = kv_grads[..., :HD]
        value_mine = kv_grads[..., HD:]
        bias_step = jnp.stack(
            [jnp.sum(query_grad, axis=(0, 1)), jnp.sum(value_mine, axis=(0, 1))], axis=1
        )
        qv_bias_grad = qv_bias_grad + bias_step.reshape(-1)
        mixed_grad = jnp.stack([query_grad, key_mine, value_mine], axis=3)
        mixed_grad = mixed_grad.reshape(tokens, 3 * heads_local * HD).astype(jnp.bfloat16)
        qkv_step = contract_rows(x_low, mixed_grad)
        input_part = times_transposed(mixed_grad, full_qkv).reshape(
            seq_local, rows_local, model_width
        )
        input_mine = lax.psum_scatter(
            input_part.astype(jnp.bfloat16), "tp", scatter_dimension=1, tiled=True
        ).astype(jnp.float32)
        first_part = pick_rows(first_grad)
        input_rows.append(input_mine + first_part)
        gain_step = jnp.stack([gain_one, gain_two], axis=1)
        shift_step = jnp.stack([shift_zero, shift_one, shift_two, shift_three], axis=1)
        full_totals = tuple(
            map(
                add_pair,
                full_totals,
                (qkv_step, out_step, up_step, down_step, gain_step, shift_step),
            )
        )
    share_totals = (
        lax.psum_scatter(
            full_totals[0].astype(jnp.bfloat16), ("fsdp", "ctx"), scatter_dimension=0, tiled=True
        ).astype(jnp.float32),
        lax.psum_scatter(
            full_totals[1].astype(jnp.bfloat16), ("fsdp", "ctx"), scatter_dimension=0, tiled=True
        ).astype(jnp.float32),
        lax.psum_scatter(
            full_totals[2].astype(jnp.bfloat16), ("fsdp", "ctx"), scatter_dimension=0, tiled=True
        ).astype(jnp.float32),
        lax.psum_scatter(
            full_totals[3].astype(jnp.bfloat16), ("fsdp", "ctx"), scatter_dimension=0, tiled=True
        ).astype(jnp.float32),
        lax.psum_scatter(
            full_totals[4].astype(jnp.bfloat16), ("fsdp", "ctx"), scatter_dimension=0, tiled=True
        ).astype(jnp.float32),
        lax.psum_scatter(
            full_totals[5].astype(jnp.bfloat16), ("fsdp", "ctx"), scatter_dimension=0, tiled=True
        ).astype(jnp.float32),
    )
    qv_total, up_total = lax.psum((qv_bias_grad, up_bias_grad), ("fsdp", "ctx"))
    return (
        jnp.stack(layer_rows, axis=0),
        jnp.stack(input_rows, axis=0),
        share_totals[0],
        qv_total,
        share_totals[1],
        share_totals[2],
        up_total,
        share_totals[3],
        share_totals[4],
        share_totals[5],
    )


def solution(mesh):
    placed = (
        P(None, "fsdp", "ctx", None),
        P(None, "fsdp", "ctx", None),
        P(None, "fsdp", None),
        P(("fsdp", "ctx"), "tp"),
        P("tp"),
        P(("fsdp", "ctx"), "tp"),
        P(("fsdp", "ctx"), "tp"),
        P("tp"),
        P(("fsdp", "ctx"), "tp"),
        P(("fsdp", "ctx"), None),
        P(("fsdp", "ctx"), None),
    )
    return jax.shard_map(
        local,
        mesh=mesh,
        in_specs=placed,
        out_specs=(
            P(None, "fsdp", ("ctx", "tp"), None),
            P(None, "fsdp", ("ctx", "tp"), None),
            P(("fsdp", "ctx"), "tp"),
            P("tp"),
            P(("fsdp", "ctx"), "tp"),
            P(("fsdp", "ctx"), "tp"),
            P("tp"),
            P(("fsdp", "ctx"), "tp"),
            P(("fsdp", "ctx"), None),
            P(("fsdp", "ctx"), None),
        ),
        check_vma=False,
    )
```

profile of v0, /device:TPU:0, one launch (start us, length us, event | category | flops | bytes accessed | tf_op | source)
XLA Modules:
  0.0 1028.2 jit_solution(4687349844855321863)
XLA Ops:
  9.5 28.8 %all-gather.6.cloned.1.call-done = bf16[1024,768]{1,0:T(8,128)(2,1)} async-done(((bf16[128,768]{1,0:T(8,128)(2,1)}), bf16[1024,768]{1,0:T(8,128)(2,1)}) %all-gather.6.cloned.1.call-update) | async-done | bytes 1572880 | tf_op jit(solution)/shard_map/all_gather | solution.py:91
  45.8 19.5 %all_gather.32 = bf16[1024,256]{1,0:T(8,128)(2,1)S(1)} all-gather(bf16[128,256]{1,0:T(8,128)(2,1)S(1)} %copy-done.39), channel_id=1, replica_groups=mesh['fsdp'=4,'ctx'=2,'tp'=4] {'fsdp','ctx'}, dimensions={0}, use_global_device_ids=true | all-gather | bytes 589824 | tf_op jit(solution)/shard_map/all_gather | solution.py:92
  75.9 17.4 %all-gather.14.cloned.1.call-done = bf16[2,512,4,128]{1,3,2,0:T(8,128)(2,1)} async-done(((bf16[2,256,4,128]{1,3,2,0:T(8,128)(2,1)}), bf16[2,512,4,128]{1,3,2,0:T(8,128)(2,1)}) %all-gather.14.cloned.1.call-update) | async-done | bytes 1048592 | tf_op jit(solution)/shard_map/all_gather | solution.py:109
  106.2 12.1 %all_gather.33 = bf16[1024,4]{0,1:T(4,128)(2,1)S(1)} all-gather(bf16[128,4]{0,1:T(4,128)(2,1)S(1)} %copy-done.41), channel_id=1, replica_groups=mesh['fsdp'=4,'ctx'=2,'tp'=4] {'fsdp','ctx'}, dimensions={0}, use_global_device_ids=true | all-gather | bytes 9216 | tf_op jit(solution)/shard_map/all_gather | solution.py:96
  118.4 10.9 %all_gather.34 = bf16[1024,2]{0,1:T(2,128)(2,1)S(1)} all-gather(bf16[128,2]{0,1:T(2,128)(2,1)S(1)} %copy-done.42), channel_id=1, replica_groups=mesh['fsdp'=4,'ctx'=2,'tp'=4] {'fsdp','ctx'}, dimensions={0}, use_global_device_ids=true | all-gather | bytes 4608 | tf_op jit(solution)/shard_map/all_gather | solution.py:95
  129.3 129.0 %all-reduce.12.cloned.1.call-done = (f32[512,1024]{1,0:T(8,128)}, f32[512,1024]{1,0:T(8,128)}) async-done(((f32[512,1024]{1,0:T(8,128)}, f32[512,1024]{1,0:T(8,128)}), (f32[512,1024]{1,0:T(8,128)}, f32[512,1024]{1,0:T(8,128)})) %all-reduce.12.cloned.1.call-update) | async-done | bytes 4194320 | tf_op jit(solution)/shard_map/psum | solution.py:49
  263.1 23.7 %all-gather.10.cloned.1.call-done = bf16[1024,1024]{1,0:T(8,128)(2,1)} async-done(((bf16[128,1024]{1,0:T(8,128)(2,1)}), bf16[1024,1024]{1,0:T(8,128)(2,1)}) %all-gather.10.cloned.1.call-update) | async-done | bytes 2097168 | tf_op jit(solution)/shard_map/all_gather | solution.py:93
  291.9 11.7 %multiply_convert_fusion.2 = (bf16[512,1024]{1,0:T(8,128)(2,1)}, f32[512,1024]{1,0:T(8,128)}, bf16[512,1024]{1,0:T(8,128)(2,1)}, f32[512,1024]{1,0:T(8,128)}, f32[512,1024]{1,0:T(8,128)}) fusion(f32[1024]{0:T(1024)S(1)} %convert_element_type.236, f32[512,1024]{1,0:T(8,128)S(1)} %fusion.124, bf16[1024,1024]{1,0:T(8,128)(2,1)S(1)} %copy-done.43, ...), kind=kOutput, calls=%fused_computation.54 | convolution fusion | flops 1145569280 | bytes 14696448 | tf_op jit(solution)/shard_map/dot_general | solution.py:131
  303.6 12.8 %all-gather.12.cloned.1.call-done = bf16[1024,1024]{1,0:T(8,128)(2,1)} async-done(((bf16[128,1024]{1,0:T(8,128)(2,1)}), bf16[1024,1024]{1,0:T(8,128)(2,1)}) %all-gather.12.cloned.1.call-update) | async-done | bytes 2097168 | tf_op jit(solution)/shard_map/all_gather | solution.py:94
  316.4 4.7 fusion.148
  324.2 154.7 %all-reduce.10.cloned.1.call-done = (f32[512,1024]{1,0:T(8,128)}, f32[512,1024]{1,0:T(8,128)}) async-done(((f32[512,1024]{1,0:T(8,128)}, f32[512,1024]{1,0:T(8,128)}), (f32[512,1024]{1,0:T(8,128)}, f32[512,1024]{1,0:T(8,128)})) %all-reduce.10.cloned.1.call-update) | async-done | bytes 4194320 | tf_op jit(solution)/shard_map/psum | solution.py:49
  478.9 4.2 fusion.132
  501.7 153.9 %all-reduce.8.cloned.1.call-done = (f32[512,1024]{1,0:T(8,128)}, f32[512,1024]{1,0:T(8,128)}) async-done(((f32[512,1024]{1,0:T(8,128)}, f32[512,1024]{1,0:T(8,128)}), (f32[512,1024]{1,0:T(8,128)}, f32[512,1024]{1,0:T(8,128)})) %all-reduce.8.cloned.1.call-update) | async-done | bytes 4194320 | tf_op jit(solution)/shard_map/psum | solution.py:49
  655.6 4.0 multiply_reduce_fusion.2
  682.9 4.0 multiply_reduce_fusion.1
  742.3 24.5 %reduce-scatter.27.cloned.1.call-done = bf16[128,1024]{1,0:T(8,128)(2,1)} async-done(((bf16[1024,1024]{1,0:T(8,128)(2,1)}), bf16[128,1024]{1,0:T(8,128)(2,1)}) %reduce-scatter.27.cloned.1.call-update) | async-done | bytes 262160 | tf_op jit(solution)/shard_map/reduce_scatter | solution.py:219
  768.5 42.5 %reduce-scatter.29.cloned.1.call-done = bf16[128,1024]{1,0:T(8,128)(2,1)} async-done(((bf16[1024,1024]{1,0:T(8,128)(2,1)}), bf16[128,1024]{1,0:T(8,128)(2,1)}) %reduce-scatter.29.cloned.1.call-update) | async-done | bytes 262160 | tf_op jit(solution)/shard_map/reduce_scatter | solution.py:222
  812.8 35.0 %reduce-scatter.33.cloned.1.call-done = bf16[128,2]{1,0:T(8,128)(2,1)} async-done(((bf16[1024,2]{1,0:T(8,128)(2,1)}), bf16[128,2]{1,0:T(8,128)(2,1)}) %reduce-scatter.33.cloned.1.call-update) | async-done | bytes 528
  849.2 35.2 %reduce-scatter.35.cloned.1.call-done = bf16[128,4]{1,0:T(8,128)(2,1)} async-done(((bf16[1024,4]{1,0:T(8,128)(2,1)}), bf16[128,4]{1,0:T(8,128)(2,1)}) %reduce-scatter.35.cloned.1.call-update) | async-done | bytes 1040
  885.8 35.7 %reduce-scatter.25.cloned.1.call-done = bf16[128,256]{1,0:T(8,128)(2,1)} async-done(((bf16[1024,256]{1,0:T(8,128)(2,1)}), bf16[128,256]{1,0:T(8,128)(2,1)}) %reduce-scatter.25.cloned.1.call-update) | async-done | bytes 65552 | tf_op jit(solution)/shard_map/reduce_scatter | solution.py:216
  923.3 14.3 %all-reduce = (f32[512]{0:T(512)}, f32[1024]{0:T(1024)}) all-reduce(f32[512]{0:T(512)S(1)} %add.309, f32[1024]{0:T(1024)S(1)} %add.312), channel_id=1, replica_groups=mesh['fsdp'=4,'ctx'=2,'tp'=4] {'fsdp','ctx'}, use_global_device_ids=true, to_apply=%region_37.38 | all-reduce | flops 1536 | bytes 12288 | tf_op jit(solution)/shard_map/psum | solution.py:232
  937.6 13.3 %reduce-scatter.23.cloned.1.call-done = bf16[2,64,1024]{2,1,0:T(8,128)(2,1)} async-done(((bf16[2,256,1024]{2,1,0:T(8,128)(2,1)}), bf16[2,64,1024]{2,1,0:T(8,128)(2,1)}) %reduce-scatter.23.cloned.1.call-update) | async-done | bytes 262160 | tf_op jit(solution)/shard_map/reduce_scatter | solution.py:198
  952.1 26.8 %reduce-scatter.19.cloned.1.call-done = bf16[2,64,1024]{2,1,0:T(8,128)(2,1)} async-done(((bf16[2,256,1024]{2,1,0:T(8,128)(2,1)}), bf16[2,64,1024]{2,1,0:T(8,128)(2,1)}) %reduce-scatter.19.cloned.1.call-update) | async-done | bytes 262160 | tf_op jit(solution)/shard_map/reduce_scatter | solution.py:198
  981.1 37.8 %reduce-scatter.31.cloned.1.call-done = bf16[128,768]{1,0:T(8,128)(2,1)} async-done(((bf16[1024,768]{1,0:T(8,128)(2,1)}), bf16[128,768]{1,0:T(8,128)(2,1)}) %reduce-scatter.31.cloned.1.call-update) | async-done | bytes 196624
  (279 shorter events, 156.0 us)
Async XLA Ops:
  7.2 33.6 %copy-start.31 = (bf16[2,2,256,1024]{3,2,1,0:T(8,128)(2,1)S(1)}, bf16[2,2,256,1024]{3,2,1,0:T(8,128)(2,1)}, u32[]{:S(2)}) copy-start(bf16[2,2,256,1024]{3,2,1,0:T(8,128)(2,1)} %param.11) | copy-start | bytes 6291460
  7.2 31.0 %all-gather.6.cloned.1.call-start = ((), (), s32[]{:S(2)}) async-start(), calls=%async_computation.10 | async-start | bytes 1769472 | tf_op jit(solution)/shard_map/all_gather | solution.py:91
  7.9 62.1 %all-gather.8.cloned.1.call-start = ((), (), s32[]{:S(2)}) async-start(), calls=%async_computation.11 | async-start | bytes 1572864 | tf_op jit(solution)/shard_map/all_gather | solution.py:109
  44.4 25.5 %copy-start.28 = (f32[2,256,4,3,64]{1,4,3,2,0:T(8,128)}, f32[2,256,4,3,64]{1,4,3,2,0:T(8,128)S(1)}, u32[]{:S(2)}) copy-start(f32[2,256,4,3,64]{1,4,3,2,0:T(8,128)S(1)} %fusion.69) | copy-start | bytes 4718596
  45.8 47.6 %all-gather.14.cloned.1.call-start = ((), (), s32[]{:S(2)}) async-start(), calls=%async_computation.14 | async-start | bytes 1572864 | tf_op jit(solution)/shard_map/all_gather | solution.py:109
  67.7 190.6 %all-reduce.12.cloned.1.call-start = ((), (), s32[]{:S(2)}) async-start(), calls=%async_computation.27 | async-start | bytes 8388608 | tf_op jit(solution)/shard_map/psum | solution.py:49
  103.1 183.7 %all-gather.10.cloned.1.call-start = ((), (), s32[]{:S(2)}) async-start(), calls=%async_computation.12 | async-start | bytes 2359296 | tf_op jit(solution)/shard_map/all_gather | solution.py:93
  103.7 212.7 %all-gather.12.cloned.1.call-start = ((), (), s32[]{:S(2)}) async-start(), calls=%async_computation.13 | async-start | bytes 2359296 | tf_op jit(solution)/shard_map/all_gather | solution.py:94
  104.3 14.0 %copy-start.42 = (bf16[128,2]{0,1:T(2,128)(2,1)S(1)}, bf16[128,2]{0,1:T(2,128)(2,1)}, u32[]{:S(2)}) copy-start(bf16[128,2]{0,1:T(2,128)(2,1)} %param.20) | copy-start | bytes 1540
  104.3 374.5 %all-reduce.10.cloned.1.call-start = ((), (), s32[]{:S(2)}) async-start(), calls=%async_computation.26 | async-start | bytes 8388608 | tf_op jit(solution)/shard_map/psum | solution.py:49
  261.7 28.8 %copy-start.5 = (f32[512,1024]{1,0:T(8,128)}, f32[512,1024]{1,0:T(8,128)S(1)}, u32[]{:S(2)}) copy-start(f32[512,1024]{1,0:T(8,128)S(1)} %get-tuple-element.83) | copy-start | bytes 6291460
  323.7 331.9 %all-reduce.8.cloned.1.call-start = ((), (), s32[]{:S(2)}) async-start(), calls=%async_computation.25 | async-start | bytes 8388608 | tf_op jit(solution)/shard_map/psum | solution.py:49
  501.4 215.0 %reduce-scatter.21.cloned.1.call-start = ((), (), s32[]{:S(2)}) async-start(), calls=%async_computation.17 | async-start | bytes 1572864 | tf_op jit(solution)/shard_map/reduce_scatter | solution.py:180
  680.3 44.0 %reduce-scatter.17.cloned.1.call-start = ((), (), s32[]{:S(2)}) async-start(), calls=%async_computation.15 | async-start | bytes 1572864 | tf_op jit(solution)/shard_map/reduce_scatter | solution.py:180
  691.8 75.0 %reduce-scatter.27.cloned.1.call-start = ((), (), s32[]{:S(2)}) async-start(), calls=%async_computation.20 | async-start | bytes 2359296 | tf_op jit(solution)/shard_map/reduce_scatter | solution.py:219
  698.5 112.5 %reduce-scatter.29.cloned.1.call-start = ((), (), s32[]{:S(2)}) async-start(), calls=%async_computation.21 | async-start | bytes 2359296 | tf_op jit(solution)/shard_map/reduce_scatter | solution.py:222
  704.9 142.9 %reduce-scatter.33.cloned.1.call-start = ((), (), s32[]{:S(2)}) async-start(), calls=%async_computation.23 | async-start | bytes 294912
  709.8 174.5 %reduce-scatter.35.cloned.1.call-start = ((), (), s32[]{:S(2)}) async-start(), calls=%async_computation.24 | async-start | bytes 294912
  710.8 210.6 %reduce-scatter.25.cloned.1.call-start = ((), (), s32[]{:S(2)}) async-start(), calls=%async_computation.19 | async-start | bytes 589824 | tf_op jit(solution)/shard_map/reduce_scatter | solution.py:216
  713.8 237.1 %reduce-scatter.23.cloned.1.call-start = ((), (), s32[]{:S(2)}) async-start(), calls=%async_computation.18 | async-start | bytes 1310720 | tf_op jit(solution)/shard_map/reduce_scatter | solution.py:198
  721.5 257.3 %reduce-scatter.19.cloned.1.call-start = ((), (), s32[]{:S(2)}) async-start(), calls=%async_computation.16 | async-start | bytes 1310720 | tf_op jit(solution)/shard_map/reduce_scatter | solution.py:198
  729.4 289.4 %reduce-scatter.31.cloned.1.call-start = ((), (), s32[]{:S(2)}) async-start(), calls=%async_computation.22 | async-start | bytes 1769472
  741.4 181.6 %copy-start.24 = (f32[2,256,4,128]{1,3,2,0:T(8,128)S(1)}, f32[2,256,4,128]{1,3,2,0:T(8,128)}, u32[]{:S(2)}) copy-start(f32[2,256,4,128]{1,3,2,0:T(8,128)} %copy-done.23) | copy-start | bytes 3145732
  741.4 181.7 %copy-start.22 = (f32[2,256,4,128]{1,3,2,0:T(8,128)S(1)}, f32[2,256,4,128]{1,3,2,0:T(8,128)}, u32[]{:S(2)}) copy-start(f32[2,256,4,128]{1,3,2,0:T(8,128)} %copy-done.21) | copy-start | bytes 3145732
  (49 other events, 143.2 us)
Sparse Core Ops, SparseCore 0:
  9.9 28.2 all-gather.5
  45.9 24.0 all-gather.7
  72.1 21.2 all-gather.13
  103.3 155.0 all-reduce.11
  260.1 26.7 all-gather.9
  288.6 27.7 all-gather.11
  323.8 155.0 all-reduce.9
  501.6 153.9 all-reduce.7
  680.4 19.3 reduce-scatter.20
  701.9 20.3 reduce-scatter.16
  725.6 41.1 reduce-scatter.26
  769.9 41.0 reduce-scatter.28
  814.0 33.6 reduce-scatter.32
  850.6 33.6 reduce-scatter.34
  887.3 34.1 reduce-scatter.24
  923.6 27.2 reduce-scatter.22
  953.0 25.7 reduce-scatter.18
  982.0 36.8 reduce-scatter.30
where the time goes:
time: 1040 us; the launch traced here: 1030 us
  waiting for transfers between devices  775 us (75%)
  matrix products  93.1 us (9%)
  blocking collectives  56.8 us (5%)
  other arithmetic  47.2 us (5%)
  local copies, waits for them, and re-layouts  38.3 us (4%)
  between operations  15.8 us (2%)
    psum x3, waiting for transfers between devices, reduce_rows(): return lax.psum(part, 'tp')  438 us
    unnamed x21, waiting for transfers between devices  110 us
    reduce_scatter x1, waiting for transfers between devices, local(): lax.psum_scatter(full_totals[3].astype(jnp.bfloat16), ('fsdp', 'ctx'), sc...  42.5 us
    reduce_scatter x2, waiting for transfers between devices, local(): lax.psum_scatter(input_part.astype(jnp.bfloat16), 'tp', scatter_dimension...  40.1 us
    reduce_scatter x1, waiting for transfers between devices, local(): lax.psum_scatter(full_totals[1].astype(jnp.bfloat16), ('fsdp', 'ctx'), sc...  35.7 us
    all_gather x1, waiting for transfers between devices, local(): lax.all_gather(w_qkv, ('fsdp', 'ctx'), axis=0, tiled=True)  28.8 us
    unnamed x121, local copies, waits for them, and re-layouts  25.1 us
    reduce_scatter x1, waiting for transfers between devices, local(): lax.psum_scatter(full_totals[2].astype(jnp.bfloat16), ('fsdp', 'ctx'), sc...  24.5 us
  transfers between devices with their start and end apart: 18, of which 16 were waited for; matrix products, arithmetic and copies ran while one was open for 10% of the time, Pallas kernels for 0%

commit v1 on v0

--- a/solution.py
+++ b/solution.py
@@ -1,6 +1,8 @@
 import jax
 import jax.numpy as jnp
 from jax import lax
+from jax.experimental import pallas as pl
+from jax.experimental.pallas import tpu as pltpu
 from jax.sharding import PartitionSpec as P
 
 HD = 64
@@ -244,6 +246,548 @@
     )
 
 
+MESH = pl.DeviceIdType.MESH
+ROW_A, ROW_D, ROW_AD, ROW_B = (0, 48), (48, 48), (0, 96), (96, 32)
+
+class Where:
+    def __init__(self):
+        fsdp = lax.axis_index("fsdp")
+        self.y = fsdp // 2
+        self.e = fsdp % 2
+        self.c = lax.axis_index("ctx")
+        self.t = lax.axis_index("tp")
+    def at(self, y=None, e=None, c=None, t=None):
+        y = self.y if y is None else y
+        e = self.e if e is None else e
+        c = self.c if c is None else c
+        t = self.t if t is None else t
+        return (2 * y + e, c, t)
+
+def when(cond, fn):
+    if cond is True:
+        fn()
+    else:
+        pl.when(cond)(fn)
+
+class Net:
+    def __init__(self, send_sems, recv_sems):
+        self.send_sems, self.recv_sems, self.count, self.pending = send_sems, recv_sems, 0, []
+    def pair(self):
+        self.count += 1
+        return self.count - 1
+    def send(self, index, cond, src, dst, device):
+        def make():
+            return pltpu.make_async_remote_copy(
+                src_ref=src(), dst_ref=dst(), send_sem=self.send_sems.at[index],
+                recv_sem=self.recv_sems.at[index], device_id=device, device_id_type=MESH)
+        when(cond, lambda: make().start())
+        self.pending.append((cond, make))
+    def recv(self, index, cond, here, device):
+        def wait():
+            pltpu.make_async_remote_copy(
+                src_ref=here(), dst_ref=here(), send_sem=self.send_sems.at[index],
+                recv_sem=self.recv_sems.at[index], device_id=device, device_id_type=MESH).wait_recv()
+        when(cond, wait)
+    def drain(self):
+        for cond, make in self.pending:
+            when(cond, lambda make=make: make().wait_send())
+
+def slots_of(w):
+    t = w.t
+    return [("own", t, True), ("l1", t - 1, t >= 1), ("r1", t + 1, t <= 2), ("l2", t - 2, t >= 2),
+            ("r2", t + 2, t <= 1), ("l3", t - 3, t >= 3), ("r3", t + 3, t <= 0)]
+
+class Gather:
+    STAGES = 7
+    def __init__(self, net, w, mine, full, c0, cn, local_sem, routes=(ROW_A, ROW_D, ROW_AD, ROW_B)):
+        self.net, self.w, self.mine, self.full, self.local_sem = net, w, mine, full, local_sem
+        self.cols = pl.ds(c0, cn)
+        self.row_a, self.row_d, self.row_ad, self.row_b = [None if r is None else pl.ds(*r) for r in routes]
+        self.slots = slots_of(w)
+        self.ids = {}
+    def id(self, key):
+        if key not in self.ids:
+            self.ids[key] = self.net.pair()
+        return self.ids[key]
+    def blk(self, tt, rows, y=None, c=None):
+        w = self.w
+        y = w.y if y is None else y
+        c = w.c if c is None else c
+        return lambda: self.full.at[tt, y, :, c, rows, self.cols]
+    def row(self, tt, rows, y=None):
+        y = self.w.y if y is None else y
+        return lambda: self.full.at[tt, y, :, :, rows, self.cols]
+    def colm(self, tt, rows, c=None):
+        c = self.w.c if c is None else c
+        return lambda: self.full.at[tt, :, :, c, rows, self.cols]
+    def plane(self, tt, rows):
+        return lambda: self.full.at[tt, :, :, :, rows, self.cols]
+    def same(self, key, cond, ref, device):
+        self.net.send(self.id(key), cond, ref, ref, device)
+    def sib(self):
+        w = self.w
+        dst = lambda: self.full.at[w.t, w.y, w.e, w.c, :, self.cols]
+        self.net.send(self.id("sib"), True, lambda: self.mine.at[1 - w.e, :, self.cols], dst, w.at(e=1 - w.e))
+        cp = pltpu.make_async_copy(self.mine.at[w.e, :, self.cols], dst(), self.local_sem)
+        cp.start()
+        self.own_copy = cp
+    def zsend(self, tag, slot, ref):
+        w = self.w
+        k = {"own": 0, "l1": 1, "r1": 1, "l2": 2, "r2": 2}[slot]
+        if slot == "own" or slot[0] == "l":
+            name, tt, ok = self.slot("own" if k == 0 else f"l{k}")
+            self.same((tag, "zr", k), (w.t < 3) if ok is True else jnp.logical_and(ok, w.t < 3), ref(tt), w.at(t=w.t + 1))
+        if slot == "own" or slot[0] == "r":
+            name, tt, ok = self.slot("own" if k == 0 else f"r{k}")
+            self.same((tag, "zl", k), (w.t > 0) if ok is True else jnp.logical_and(ok, w.t > 0), ref(tt), w.at(t=w.t - 1))
+    def zrecv(self, tag, slot, ref):
+        w = self.w
+        k = int(slot[1])
+        _, tt, ok = self.slot(slot)
+        if slot[0] == "l":
+            self.net.recv(self.id((tag, "zr", k - 1)), ok, ref(tt), w.at(t=w.t - 1))
+        else:
+            self.net.recv(self.id((tag, "zl", k - 1)), ok, ref(tt), w.at(t=w.t + 1))
+    def slot(self, name):
+        return next(s for s in self.slots if s[0] == name)
+    def first_hop(self, name):
+        w = self.w
+        _, tt, ok = self.slot(name)
+        self.same(("ax", name), ok, self.blk(tt, self.row_a), w.at(c=1 - w.c))
+        if self.row_d is not None:
+            self.same(("dy", name), ok, self.blk(tt, self.row_d), w.at(y=1 - w.y))
+    def second_hop(self, name):
+        w = self.w
+        _, tt, ok = self.slot(name)
+        self.net.recv(self.id(("ax", name)), ok, self.blk(tt, self.row_a, c=1 - w.c), w.at(c=1 - w.c))
+        self.same(("ay", name), ok, self.row(tt, self.row_a), w.at(y=1 - w.y))
+        if self.row_d is not None:
+            self.net.recv(self.id(("dy", name)), ok, self.blk(tt, self.row_d, y=1 - w.y), w.at(y=1 - w.y))
+            self.same(("dx", name), ok, self.colm(tt, self.row_d), w.at(c=1 - w.c))
+    def last(self, name):
+        w = self.w
+        _, tt, ok = self.slot(name)
+        self.net.recv(self.id(("ay", name)), ok, self.row(tt, self.row_a, y=1 - w.y), w.at(y=1 - w.y))
+        if self.row_d is not None:
+            self.net.recv(self.id(("dx", name)), ok, self.colm(tt, self.row_d, c=1 - w.c), w.at(c=1 - w.c))
+    def stage(self, k):
+        w = self.w
+        ad = lambda tt: self.blk(tt, self.row_ad)
+        bz = lambda tt: self.plane(tt, self.row_b)
+        b = self.row_b is not None
+        if k == 0:
+            self.sib()
+        elif k == 1:
+            self.own_copy.wait()
+            self.net.recv(self.id("sib"), True, lambda: self.full.at[w.t, w.y, 1 - w.e, w.c, :, self.cols], w.at(e=1 - w.e))
+            self.zsend("ad", "own", ad)
+            if b:
+                self.same("bx", True, self.blk(w.t, self.row_b), w.at(c=1 - w.c))
+            self.first_hop("own")
+        elif k == 2:
+            if b:
+                self.net.recv(self.id("bx"), True, self.blk(w.t, self.row_b, c=1 - w.c), w.at(c=1 - w.c))
+                self.same("by", True, self.row(w.t, self.row_b), w.at(y=1 - w.y))
+            for s in ("l1", "r1"):
+                self.zrecv("ad", s, ad)
+                self.zsend("ad", s, ad)
+                self.first_hop(s)
+            self.second_hop("own")
+        elif k == 3:
+            if b:
+                self.net.recv(self.id("by"), True, self.row(w.t, self.row_b, y=1 - w.y), w.at(y=1 - w.y))
+                self.zsend("b", "own", bz)
+            for s in ("l2", "r2"):
+                self.zrecv("ad", s, ad)
+                self.zsend("ad", s, ad)
+                self.first_hop(s)
+            for s in ("l1", "r1"):
+                self.second_hop(s)
+        elif k == 4:
+            if b:
+                for s in ("l1", "r1"):
+                    self.zrecv("b", s, bz)
+                    self.zsend("b", s, bz)
+            for s in ("l3", "r3"):
+                self.zrecv("ad", s, ad)
+                self.first_hop(s)
+            for s in ("l2", "r2"):
+                self.second_hop(s)
+        elif k == 5:
+            if b:
+                for s in ("l2", "r2"):
+                    self.zrecv("b", s, bz)
+                    self.zsend("b", s, bz)
+            for s in ("l3", "r3"):
+                self.second_hop(s)
+        elif k == 6:
+            if b:
+                for s in ("l3", "r3"):
+                    self.zrecv("b", s, bz)
+            for name, _, _ in self.slots:
+                self.last(name)
+
+def barrier(w, extra=()):
+    sem = pltpu.get_barrier_semaphore()
+    one = lambda dev: pl.semaphore_signal(sem, inc=1, device_id=dev, device_id_type=MESH)
+    one(w.at(e=1 - w.e)); one(w.at(c=1 - w.c)); one(w.at(y=1 - w.y))
+    pl.when(w.t > 0)(lambda: one(w.at(t=w.t - 1)))
+    pl.when(w.t < 3)(lambda: one(w.at(t=w.t + 1)))
+    ends = jnp.where(w.t == 0, 1, 0) + jnp.where(w.t == 3, 1, 0)
+    return sem, one, 5 - ends
+
+def gather_kernel(mine, small, x_in, g_in, full, small_full, x_all, g_own, send_sems, recv_sems, local_sems):
+    w = Where()
+    sem, one, need = barrier(w)
+    cross = w.e != w.c
+    diag = w.at(e=1 - w.e, c=1 - w.c)
+    pl.when(cross)(lambda: one(diag))
+    pl.semaphore_wait(sem, need + jnp.where(cross, 1, 0))
+    net = Net(send_sems, recv_sems)
+    seq = lambda ref: ref.at[w.t // 2, w.t % 2]
+    parts = [Gather(net, w, small, small_full, 0, 128, local_sems.at[0], routes=((0, 16), None, (0, 16), None))]
+    parts += [Gather(net, w, mine, full, 512 * i, 512, local_sems.at[1 + i]) for i in range(3)]
+    xi, gi, xs = net.pair(), net.pair(), net.pair()
+    parts[1].stage(0)
+    parts[0].stage(0)
+    for idx, src, dst in ((xi, x_in, x_all.at[0]), (gi, g_in, g_own)):
+        net.send(idx, cross, lambda src=src: seq(src), lambda dst=dst: dst, diag)
+    local = [pltpu.make_async_copy(seq(x_in), x_all.at[0], local_sems.at[4]),
+             pltpu.make_async_copy(seq(g_in), g_own, local_sems.at[5])]
+    for cp in local:
+        pl.when(jnp.logical_not(cross))(lambda cp=cp: cp.start())
+    parts[2].stage(0)
+    parts[3].stage(0)
+    parts[1].stage(1)
+    parts[0].stage(1)
+    pl.when(jnp.logical_not(cross))(lambda: local[0].wait())
+    net.recv(xi, cross, lambda: x_all.at[0], diag)
+    net.send(xs, True, lambda: x_all.at[0], lambda: x_all.at[1], w.at(e=1 - w.e))
+    for s in range(2, 12):
+        for i, start in ((1, 0), (0, 0), (2, 2), (3, 4)):
+            k = s - start
+            if 1 <= k <= 6:
+                parts[i].stage(k)
+    pl.when(jnp.logical_not(cross))(lambda: local[1].wait())
+    net.recv(gi, cross, lambda: g_own, diag)
+    net.recv(xs, True, lambda: x_all.at[1], w.at(e=1 - w.e))
+    net.drain()
+
+N_GATHER = 153
+
+def run_gather(mine, small, x_in, g_in):
+    any_ = pl.BlockSpec(memory_space=pl.ANY)
+    vm = pl.BlockSpec(memory_space=pltpu.VMEM)
+    rows, width = x_in.shape[2:]
+    return pl.pallas_call(
+        gather_kernel,
+        out_shape=(jax.ShapeDtypeStruct((4, 2, 2, 2) + mine.shape[1:], mine.dtype),
+                   jax.ShapeDtypeStruct((4, 2, 2, 2) + small.shape[1:], small.dtype),
+                   jax.ShapeDtypeStruct((2, rows, width), x_in.dtype),
+                   jax.ShapeDtypeStruct((rows, width), g_in.dtype)),
+        in_specs=[vm, vm, vm, vm],
+        out_specs=(any_, any_, any_, any_),
+        scratch_shapes=[pltpu.SemaphoreType.DMA((N_GATHER,)), pltpu.SemaphoreType.DMA((N_GATHER,)), pltpu.SemaphoreType.DMA((6,))],
+        compiler_params=pltpu.CompilerParams(collective_id=0, has_side_effects=True),
+        name="gather",
+    )(mine, small, x_in, g_in)
+
+
+ROWS = {"a": pl.ds(0, 48), "d": pl.ds(48, 48), "ad": pl.ds(0, 96), "b": pl.ds(96, 32)}
+
+class Scatter:
+    def __init__(self, net, w, g, bufs, c0, cn):
+        self.net, self.w, self.g, self.bufs = net, w, g, bufs
+        self.cols = pl.ds(c0, cn)
+        self.ids = {}
+    def id(self, key):
+        if key not in self.ids:
+            self.ids[key] = self.net.pair()
+        return self.ids[key]
+    def take(self, key, cond, buf, place, device):
+        cols = self.cols
+        def body():
+            self.net.recv(self.id(key), True, lambda: buf(), device)
+            ref = place()
+            ref[...] = (ref[...].astype(jnp.float32) + buf()[...].astype(jnp.float32)).astype(ref.dtype)
+        when(cond, body)
+    def zstep(self, tag, m, place):
+        w = self.w
+        for way, me, targets in (("r", m, [j for j in (3, 2, 1) if j >= m]), ("l", 3 - m, [j for j in (0, 1, 2) if j <= 3 - m])):
+            buf = self.bufs[tag + "z" + way]
+            nxt = w.at(t=w.t + 1) if way == "r" else w.at(t=w.t - 1)
+            prv = w.at(t=w.t - 1) if way == "r" else w.at(t=w.t + 1)
+            here = w.t == me
+            for j in targets:
+                land = lambda j=j, buf=buf: buf.at[j, ..., self.cols]
+                if m > 0:
+                    self.take((tag, way, j), here, land, place(j), prv)
+                if j != me:
+                    self.net.send(self.id((tag, way, j)), here, place(j), land, nxt)
+    def stage(self, k):
+        w, g, cols, b = self.w, self.g, self.cols, self.bufs
+        X, Y = w.at(c=1 - w.c), w.at(y=1 - w.y)
+        ad = lambda j: (lambda: g.at[j, w.y, :, w.c, ROWS["ad"], cols])
+        bz = lambda j: (lambda: g.at[j, :, :, :, ROWS["b"], cols])
+        order = (3, 0, 2, 1)
+        if k == 0:
+            self.zstep("b", 0, bz)
+            for j in order:
+                self.net.send(self.id(("ya", j)), True, lambda j=j: g.at[j, 1 - w.y, :, :, ROWS["a"], cols], lambda j=j: b["ya"].at[j, :, :, :, cols], Y)
+                self.net.send(self.id(("xd", j)), True, lambda j=j: g.at[j, :, :, 1 - w.c, ROWS["d"], cols], lambda j=j: b["xd"].at[j, :, :, :, cols], X)
+        elif k == 1:
+            self.zstep("b", 1, bz)
+            for j in order:
+                self.take(("ya", j), True, lambda j=j: b["ya"].at[j, :, :, :, cols], lambda j=j: g.at[j, w.y, :, :, ROWS["a"], cols], Y)
+                self.net.send(self.id(("xa", j)), True, lambda j=j: g.at[j, w.y, :, 1 - w.c, ROWS["a"], cols], lambda j=j: b["xa"].at[j, :, :, cols], X)
+                self.take(("xd", j), True, lambda j=j: b["xd"].at[j, :, :, :, cols], lambda j=j: g.at[j, :, :, w.c, ROWS["d"], cols], X)
+                self.net.send(self.id(("yd", j)), True, lambda j=j: g.at[j, 1 - w.y, :, w.c, ROWS["d"], cols], lambda j=j: b["yd"].at[j, :, :, cols], Y)
+        elif k == 2:
+            self.zstep("b", 2, bz)
+            for j in order:
+                self.take(("xa", j), True, lambda j=j: b["xa"].at[j, :, :, cols], lambda j=j: g.at[j, w.y, :, w.c, ROWS["a"], cols], X)
+                self.take(("yd", j), True, lambda j=j: b["yd"].at[j, :, :, cols], lambda j=j: g.at[j, w.y, :, w.c, ROWS["d"], cols], Y)
+            self.zstep("ad", 0, ad)
+        elif k == 3:
+            self.zstep("b", 3, bz)
+            self.net.send(self.id("by"), True, lambda: g.at[w.t, 1 - w.y, :, :, ROWS["b"], cols], lambda: b["by"].at[:, :, :, cols], Y)
+            self.zstep("ad", 1, ad)
+        elif k == 4:
+            self.take("by", True, lambda: b["by"].at[:, :, :, cols], lambda: g.at[w.t, w.y, :, :, ROWS["b"], cols], Y)
+            self.net.send(self.id("bx"), True, lambda: g.at[w.t, w.y, :, 1 - w.c, ROWS["b"], cols], lambda: b["bx"].at[:, :, cols], X)
+            self.zstep("ad", 2, ad)
+        elif k == 5:
+            self.zstep("ad", 3, ad)
+            self.take("bx", True, lambda: b["bx"].at[:, :, cols], lambda: g.at[w.t, w.y, :, w.c, ROWS["b"], cols], X)
+            self.net.send(self.id("sib"), True, lambda: g.at[w.t, w.y, 1 - w.e, w.c, :, cols], lambda: b["sib"].at[:, cols], w.at(e=1 - w.e))
+        elif k == 6:
+            self.net.recv(self.id("sib"), True, lambda: b["sib"].at[:, cols], w.at(e=1 - w.e))
+
+PIECES = ((0, 384), (384, 128), (512, 512), (1024, 512))
+
+def scatter_kernel(g_in, lo, ig, o_qkv, o_out, o_up, o_down, lo_out, ig_out, g, ya, xa, xd, yd, adzr, adzl, bzr, bzl, by, bx, sib, send_sems, recv_sems, local_sems):
+    w = Where()
+    sem, one, need = barrier(w)
+    same = w.e == w.c
+    for d in range(4):
+        go = (lambda d=d: one(w.at(e=w.c, c=w.e, t=(w.t + d) % 4)))
+        when(True if d else jnp.logical_not(same), go)
+    pl.semaphore_wait(sem, need + 3 + jnp.where(same, 0, 1))
+    net = Net(send_sems, recv_sems)
+    bufs = {"ya": ya, "xa": xa, "xd": xd, "yd": yd, "adzr": adzr, "adzl": adzl, "bzr": bzr, "bzl": bzl, "by": by, "bx": bx, "sib": sib}
+    ranges = (1024, 512, 0)
+    copies = [pltpu.make_async_copy(g_in.at[..., pl.ds(c0, 512)], g.at[..., pl.ds(c0, 512)], local_sems.at[i]) for i, c0 in enumerate(ranges)]
+    for cp in copies:
+        cp.start()
+    parts = [Scatter(net, w, g, bufs, c0, 512) for c0 in ranges]
+    ids = [[net.pair(), net.pair()] for _ in range(4)]
+    def rows_out(k, src, dst, local):
+        for d in range(4):
+            t2 = (w.t + d) % 4
+            here = lambda t2=t2: src.at[pl.ds(pl.multiple_of(t2 * 64, 64), 64)]
+            there = lambda: dst.at[w.t // 2, w.t % 2]
+            net.send(ids[d][k], True if d else jnp.logical_not(same), here, there, w.at(e=w.c, c=w.e, t=t2))
+        cp = pltpu.make_async_copy(src.at[pl.ds(pl.multiple_of(w.t * 64, 64), 64)], dst.at[w.t // 2, w.t % 2], local)
+        pl.when(same)(lambda: cp.start())
+        return cp
+    def rows_in(k, dst):
+        for d in range(4):
+            t2 = (w.t + 4 - d) % 4
+            net.recv(ids[d][k], True if d else jnp.logical_not(same), lambda t2=t2: dst.at[t2 // 2, t2 % 2], w.at(e=w.c, c=w.e, t=t2))
+    own = []
+    def finish(p):
+        for (c0, cn), ref in zip(PIECES, (o_qkv, o_out, o_up, o_down)):
+            if ranges[p] <= c0 < ranges[p] + 512:
+                cols = pl.ds(c0, cn)
+                ref[:, pl.ds(pl.multiple_of(w.e * cn, 128), cn)] = g[w.t, w.y, w.e, w.c, :, cols].astype(jnp.float32)
+                ref[:, pl.ds(pl.multiple_of((1 - w.e) * cn, 128), cn)] = sib[:, cols].astype(jnp.float32)
+    for s in range(11):
+        for p, start in ((0, 0), (1, 2), (2, 4)):
+            k = s - start
+            if 0 <= k <= 6:
+                if k == 0:
+                    copies[p].wait()
+                parts[p].stage(k)
+                if k == 6:
+                    finish(p)
+        if s == 0:
+            own.append(rows_out(0, lo, lo_out, local_sems.at[3]))
+        if s == 2:
+            own.append(rows_out(1, ig, ig_out, local_sems.at[4]))
+    for cp in own:
+        pl.when(same)(lambda cp=cp: cp.wait())
+    rows_in(0, lo_out)
+    rows_in(1, ig_out)
+    net.drain()
+
+N_SCATTER = 101
+
+def run_scatter(g, lo, ig):
+    any_ = pl.BlockSpec(memory_space=pl.ANY)
+    vm = pl.BlockSpec(memory_space=pltpu.VMEM)
+    f32, bf = jnp.float32, jnp.bfloat16
+    n = g.shape[-1]
+    share = lo.shape[0] // 4
+    sd = jax.ShapeDtypeStruct
+    return pl.pallas_call(
+        scatter_kernel,
+        out_shape=(sd((128, 768), f32), sd((128, 256), f32), sd((128, 1024), f32), sd((128, 1024), f32),
+                   sd((2, 2, share, lo.shape[1]), lo.dtype), sd((2, 2, share, ig.shape[1]), ig.dtype)),
+        in_specs=[any_, vm, vm],
+        out_specs=(vm, vm, vm, vm, any_, any_),
+        scratch_shapes=[pltpu.VMEM(g.shape, bf),
+                        pltpu.VMEM((4, 2, 2, 48, n), bf), pltpu.VMEM((4, 2, 48, n), bf),
+                        pltpu.VMEM((4, 2, 2, 48, n), bf), pltpu.VMEM((4, 2, 48, n), bf),
+                        pltpu.VMEM((4, 2, 96, n), bf), pltpu.VMEM((4, 2, 96, n), bf),
+                        pltpu.VMEM((4, 2, 2, 2, 32, n), bf), pltpu.VMEM((4, 2, 2, 2, 32, n), bf),
+                        pltpu.VMEM((2, 2, 32, n), bf), pltpu.VMEM((2, 32, n), bf), pltpu.VMEM((128, n), bf),
+                        pltpu.SemaphoreType.DMA((N_SCATTER,)), pltpu.SemaphoreType.DMA((N_SCATTER,)), pltpu.SemaphoreType.DMA((5,))],
+        compiler_params=pltpu.CompilerParams(collective_id=1, has_side_effects=True),
+        name="scatter",
+    )(g, lo, ig)
+
+
+def swap_cores(value):
+    return lax.ppermute(value, "fsdp", [(i, i ^ 1) for i in range(lax.axis_size("fsdp"))])
+
+
+def own_rows(part):
+    half = part.shape[0] // 2
+    return part[:half] + swap_cores(part[half:].astype(jnp.bfloat16)).astype(jnp.float32)
+
+
+def both_rows(rows_mine):
+    return jnp.concatenate([rows_mine, swap_cores(rows_mine)], axis=0)
+
+
+def dot32(spec, left, right):
+    return jnp.einsum(spec, left, right, preferred_element_type=jnp.float32)
+
+
+def fast_local(
+    inputs, out_grad, segment_ids, w_qkv, bias_qv, w_out, w_up, bias_up, w_down, gains, shifts
+):
+    w = Where()
+    bf, f32 = jnp.bfloat16, jnp.float32
+    rows, model_width = inputs.shape[2:]
+    tokens = 2 * rows
+    score_scale = HD ** (-0.5)
+    halves = [a.reshape(128, 2, -1) for a in (w_qkv, w_out, w_up, w_down)]
+    mine = jnp.concatenate(halves, axis=-1).transpose(1, 0, 2)
+    norms_in = jnp.concatenate([gains, shifts], axis=1).T
+    small = jnp.concatenate(
+        [
+            jnp.broadcast_to(norms_in, (2, 6, 128)),
+            bias_qv.reshape(2, 2, 128),
+            bias_up.reshape(2, 4, 128),
+            jnp.zeros((2, 4, 128), bf),
+        ],
+        axis=1,
+    )
+    ids_other = swap_cores(segment_ids)
+    full, small_full, x_all, upstream = run_gather(mine, small, inputs, out_grad)
+    full = full.reshape(4, model_width, -1)
+    small_full = small_full.reshape(4, 8, 16, 128)
+    norm_all = small_full[0, :, :6].transpose(1, 0, 2).reshape(6, model_width).astype(f32)
+    gain_rows, shift_rows = norm_all[:2], norm_all[2:]
+    qv_bias = small_full[:, 0, 6:8].astype(f32).reshape(4, 1, 2, 2, HD)
+    up_bias = small_full[:, 0, 8:12].astype(f32).reshape(4, 1, -1)
+    full_qkv, full_out, full_up, full_down = (full[:, :, c0 : c0 + cn] for c0, cn in PIECES)
+
+    ids = jnp.where(w.e == w.c, segment_ids, ids_other).reshape(4, 2, rows)
+    ids = lax.dynamic_index_in_dim(ids, w.t, 0, keepdims=False)
+    ids = jnp.where(w.e == 0, ids, ids[::-1]).reshape(tokens)
+    same_segment = ids[:, None] == ids[None, :]
+
+    x_low = x_all.reshape(tokens, model_width)
+    projected = dot32("nk,tkc->tnc", x_low, full_qkv).reshape(4, tokens, 2, 3, HD)
+    queries = (projected[:, :, :, 0] + qv_bias[:, :, :, 0]).astype(bf)
+    key_rows = projected[:, :, :, 1].astype(bf)
+    value_rows = (projected[:, :, :, 2] + qv_bias[:, :, :, 1]).astype(bf)
+
+    def get_scores():
+        scores = dot32("tqhe,tkhe->thqk", queries, key_rows) * score_scale
+        return jnp.where(same_segment, scores, masked_score)
+
+    scores = get_scores()
+    row_max = jnp.max(scores, axis=-1, keepdims=True)
+    weights = jnp.exp(scores - row_max)
+    row_total = jnp.sum(weights, axis=-1, keepdims=True)
+    probabilities = weights / row_total
+    p_low = probabilities.astype(bf)
+    attended_low = dot32("thqk,tkhe->tqhe", p_low, value_rows).astype(bf).reshape(4, tokens, 128)
+    attention_part = dot32("tnc,tkc->nk", attended_low, full_out)
+    first_sum = x_all[0].astype(f32) + own_rows(attention_part) + shift_rows[0]
+    first_norm, first_back = jax.vjp(norm_rows, first_sum, gain_rows[0], shift_rows[1])
+    norm_low = both_rows(first_norm.astype(bf))
+    before_act = dot32("nk,tkc->tnc", norm_low, full_up) + up_bias
+    activated, gelu_back = jax.vjp(exact_gelu, before_act)
+    hidden = activated.astype(bf)
+    down_part = dot32("tnc,tkc->nk", hidden, full_down)
+    second_sum = first_norm + own_rows(down_part) + shift_rows[2]
+    result, second_back = jax.vjp(norm_rows, second_sum, gain_rows[1], shift_rows[3])
+    layer_mine = result.astype(bf)
+    second_grad, gain_two, shift_three = second_back(upstream.astype(f32))
+    shift_two = jnp.sum(second_grad, axis=0)
+    second_low = both_rows(second_grad.astype(bf))
+    down_step = dot32("nk,tnc->tkc", second_low, hidden)
+    hidden_grad = dot32("nk,tkc->tnc", second_low, full_down)
+    (act_grad,) = gelu_back(hidden_grad)
+    up_bias_grad = jnp.sum(act_grad, axis=1)
+    act_low = act_grad.astype(bf)
+    up_step = dot32("nk,tnc->tkc", norm_low, act_low)
+    back_part = dot32("tnc,tkc->nk", act_low, full_up)
+    norm_grad = second_grad + own_rows(back_part)
+    first_grad, gain_one, shift_one = first_back(norm_grad)
+    shift_zero = jnp.sum(first_grad, axis=0)
+    first_low = both_rows(first_grad.astype(bf))
+    out_step = dot32("nk,tnc->tkc", first_low, attended_low)
+    attended_grad = dot32("nk,tkc->tnc", first_low, full_out).astype(bf).reshape(4, tokens, 2, HD)
+    value_grad = dot32("thqk,tqhe->tkhe", p_low, attended_grad)
+    prob_grad = dot32("tqhe,tkhe->thqk", attended_grad, value_rows)
+    row_dot = jnp.sum(prob_grad * probabilities, axis=-1, keepdims=True)
+    score_grad = (probabilities * (prob_grad - row_dot)).astype(bf)
+    query_grad = dot32("thqk,tkhe->tqhe", score_grad, key_rows) * score_scale
+    key_grad = dot32("thqk,tqhe->tkhe", score_grad, queries) * score_scale
+    qv_grad = jnp.stack([jnp.sum(query_grad, axis=1), jnp.sum(value_grad, axis=1)], axis=2)
+    mixed_grad = jnp.stack([query_grad, key_grad, value_grad], axis=3).astype(bf)
+    mixed_grad = mixed_grad.reshape(4, tokens, 6 * HD)
+    qkv_step = dot32("nk,tnc->tkc", x_low, mixed_grad)
+    input_part = dot32("tnc,tkc->nk", mixed_grad, full_qkv)
+    input_mine = (first_grad + own_rows(input_part)).astype(bf)
+
+    norm_sums = jnp.stack([gain_one, gain_two, shift_zero, shift_one, shift_two, shift_three])
+    head_sums = jnp.concatenate([qv_grad.reshape(4, 256), up_bias_grad.reshape(4, 512)], axis=1)
+    head_sums = jnp.stack([jnp.where(w.e == i, head_sums, 0.0) for i in range(2)])
+    norm_sums, head_sums = lax.psum((norm_sums, head_sums), ("fsdp", "ctx", "tp"))
+    head_mine = lax.dynamic_index_in_dim(head_sums, w.t, 1, keepdims=False)
+    block = (2 * w.y + w.e) * 2 + w.c
+    norm_mine = lax.dynamic_slice_in_dim(norm_sums, block * 128, 128, 1)
+
+    steps = jnp.concatenate(
+        [a.astype(bf) for a in (qkv_step, out_step, up_step, down_step)], axis=-1
+    )
+    g_qkv, g_out, g_up, g_down, layer_out, input_out = run_scatter(
+        steps.reshape(4, 2, 2, 2, 128, -1), layer_mine, input_mine
+    )
+    return (
+        layer_out,
+        input_out.astype(f32),
+        g_qkv,
+        head_mine[:, :256].reshape(-1),
+        g_out,
+        g_up,
+        head_mine[:, 256:].reshape(-1),
+        g_down,
+        norm_mine[:2].T,
+        norm_mine[2:].T,
+    )
+
+
+def fits_fast(mesh):
+    return dict(mesh.shape) == {"fsdp": 4, "ctx": 2, "tp": 4}
+
+
 def solution(mesh):
     placed = (
         P(None, "fsdp", "ctx", None),
@@ -259,7 +803,7 @@
         P(("fsdp", "ctx"), None),
     )
     return jax.shard_map(
-        local,
+        fast_local if fits_fast(mesh) else local,
         mesh=mesh,
         in_specs=placed,
         out_specs=(

time: 1040 us -> 436 us (0.42)
  waiting for transfers between devices: 775 us -> 7.72 us
  Pallas kernels: 0 us -> 249 us
  matrix products: 93.1 us -> 69 us
  other arithmetic: 47.2 us -> 24.4 us
  blocking collectives: 56.8 us -> 38.8 us
  between operations: 15.8 us -> 1.9 us
    psum x3 -> x0, waiting for transfers between devices: 438 us -> none  [reduce_rows(): return lax.psum(part, 'tp')]
    pallas_call x0 -> x2, Pallas kernels: none -> 249 us  [the longest x1 136 us: run_scatter(): pl.pallas_call(scatter_kernel, out_shape=(sd((128, 768), f32), sd((128, 2...]
    reduce_scatter x7 -> x0, waiting for transfers between devices: 143 us -> none  [the longest x1 42.5 us: local(): lax.psum_scatter(full_totals[3].astype(jnp.bfloat16), ('fsdp', 'ctx'), sc...]
    unnamed x21 -> x0, waiting for transfers between devices: 110 us -> none
    all_gather x5 -> x0, waiting for transfers between devices: 85 us -> none  [the longest x1 28.8 us: local(): lax.all_gather(w_qkv, ('fsdp', 'ctx'), axis=0, tiled=True)]
    all_gather x3 -> x0, blocking collectives: 42.5 us -> none  [the longest x1 19.5 us: local(): lax.all_gather(w_out, ('fsdp', 'ctx'), axis=0, tiled=True)]
    dot_general x36 -> x17, matrix products: 93.1 us -> 61.4 us  [dot32(): return jnp.einsum(spec, left, right, preferred_element_type=jnp.float32)]
    psum x1, blocking collectives: 14.3 us -> 38.8 us  [fast_local(): lax.psum((norm_sums, head_sums), ('fsdp', 'ctx', 'tp'))]
  transfers between devices with their start and end apart: 18 -> 8, of which waited for: 16 -> 5; matrix products, arithmetic and copies ran while one was open for 10% -> 12% of each run, Pallas kernels for 0% -> 26%
where the time goes in v1:
time: 436 us; the launch traced here: 431 us
  Pallas kernels  249 us (57%)
  matrix products  69 us (16%)
  blocking collectives  38.8 us (9%)
  local copies, waits for them, and re-layouts  38.4 us (9%)
  other arithmetic  24.4 us (6%)
  waiting for transfers between devices  7.72 us (2%)
    pallas_call x1, Pallas kernels, run_scatter(): pl.pallas_call(scatter_kernel, out_shape=(sd((128, 768), f32), sd((128, 2...  136 us
    pallas_call x1, Pallas kernels, run_gather(): pl.pallas_call(gather_kernel, out_shape=(jax.ShapeDtypeStruct((4, 2, 2, 2...  112 us
    dot_general x17, matrix products, dot32(): return jnp.einsum(spec, left, right, preferred_element_type=jnp.float32)  61.4 us
    psum x1, blocking collectives, fast_local(): lax.psum((norm_sums, head_sums), ('fsdp', 'ctx', 'tp'))  38.8 us
    concatenate x1, local copies, waits for them, and re-layouts, fast_local(): jnp.concatenate([a.astype(bf) for a in (qkv_step, out_step, up_step, down...  16.6 us
    unnamed x84, local copies, waits for them, and re-layouts  16 us
  transfers between devices with their start and end apart: 8, of which 5 were waited for; matrix products, arithmetic and copies ran while one was open for 12% of the time, Pallas kernels for 26%

profile of v1, /device:TPU:0, one launch (start us, length us, event | category | flops | bytes accessed | tf_op | source)
XLA Modules:
  0.0 430.8 jit_solution(14269514992260187851)
XLA Ops:
  8.5 112.5 %gather.1 = (bf16[4,2,2,2,128,1536]{5,4,3,2,1,0:T(8,128)(2,1)}, bf16[4,2,2,2,16,128]{5,4,3,2,1,0:T(8,128)(2,1)}, bf16[2,256,1024]{2,1,0:T(8,128)(2,1)}, bf16[256,1024]{1,0:T(8,128)(2,1)}) custom-call(bf16[2,128,1536]{2,1,0:T(8,128)(2,1)} %maximum_bitcast_fusion.3.mine, bf16[2,16,128]{2,1,0:T(8,128)(2,1)} %maximum_maximum_fusion.small, ...), custom_call_target="tpu_custom_call" | custom-call | tf_op jit(solution)/shard_map/gather/pallas_call | solution.py:482
  121.0 4.0 fusion.34
  128.7 7.6 %fusion.112 = (f32[4,2,512]{2,1,0:T(2,128)S(1)}, f32[4,2,512,512]{2,3,1,0:T(8,128)}) fusion(pred[512,512]{0,1:T(8,128)(4,1)S(1)} %broadcast_compare_fusion, f32[4,512,2,1,64]{1,4,3,2,0:T(8,128)} %get-tuple-element.49, f32[4,2,64]{2,1,0:T(2,128)S(1)} %bitcast.301, f32[4,512,2,3,64]{1,4,3,2,0:T(8,128)S(1)} %bitcast.257), kind=kOutput, calls=%fused_computation.175 | convolution fusion | flops 277348864 | bytes 10244096 | tf_op jit(solution)/shard_map/sub | solution.py:714
  136.4 4.7 %fusion.55 = bf16[4,2,64,512]{3,2,1,0:T(8,128)(2,1)S(1)} fusion(f32[4,512,2,1,64]{1,4,3,2,0:T(8,128)} %get-tuple-element.50, f32[4,2,64]{2,1,0:T(2,128)S(1)} %bitcast.308, f32[4,2,512,512]{2,3,1,0:T(8,128)} %get-tuple-element.67, f32[4,2,512]{2,1,0:T(2,128)S(1)} %get-tuple-element.66), kind=kOutput, calls=%fused_computation.75 | convolution fusion | flops 273416192 | bytes 9979904 | tf_op jit(solution)/shard_map/thqk,tkhe->tqhe/dot_general | solution.py:664
  141.1 2.8 convolution_bitcast_fusion
  148.8 11.0 %fusion.10 = (bf16[4,512,512]{2,1,0:T(8,128)(2,1)S(1)}, f32[4,512,512]{2,1,0:T(8,128)S(1)}, f32[4,512,512]{1,2,0:T(8,128)S(1)}) fusion(f32[4,512]{1,0:T(4,128)S(1)} %bitcast.305, bf16[4,1024,1536]{2,1,0:T(8,128)(2,1)S(1)} %bitcast.281, bf16[256,1024]{1,0:T(8,128)(2,1)S(1)} %collective-permute-done.2, bf16[256,1024]{1,0:T(8,128)(2,1)S(1)} %fusion.79), kind=kOutput, calls=%fused_computation.23 | convolution fusion | flops 2218786816 | bytes 15736832 | tf_op jit(solution)/shard_map/nk,tkc->tnc/dot_general | solution.py:664
  159.9 2.4 fusion.47
  169.0 4.1 fusion.117
  173.1 2.4 fusion.44
  177.8 2.0 collective-permute-done.5
  183.1 4.4 %convert_bitcast_fusion.1 = bf16[4,1024,512]{1,2,0:T(8,128)(2,1)} fusion(bf16[4,512,512]{2,1,0:T(8,128)(2,1)S(1)} %copy-done.28, bf16[256,1024]{1,0:T(8,128)(2,1)S(1)} %copy-done.22, bf16[256,1024]{1,0:T(8,128)(2,1)S(1)} %copy-done.11), kind=kOutput, calls=%fused_computation.25 | convolution fusion | flops 2151677952 | bytes 7340032 | tf_op jit(solution)/shard_map/nk,tnc->tkc/dot_general | solution.py:664
  187.5 4.3 %convert_bitcast_fusion = bf16[4,1024,512]{1,2,0:T(8,128)(2,1)} fusion(bf16[4,512,512]{2,1,0:T(8,128)(2,1)S(1)} %copy-done.26, bf16[256,1024]{1,0:T(8,128)(2,1)S(1)} %copy-done.24, bf16[256,1024]{1,0:T(8,128)(2,1)S(1)} %copy-done.14), kind=kOutput, calls=%fused_computation.24 | convolution fusion | flops 2151677952 | bytes 7340032 | tf_op jit(solution)/shard_map/nk,tnc->tkc/dot_general | solution.py:664
  191.9 2.4 convolution_convert_fusion.1
  194.4 4.6 %multiply_reduce_fusion = (f32[4,2,512]{2,1,0:T(2,128)S(1)}, f32[4,2,512,512]{2,3,1,0:T(8,128)S(1)}) fusion(f32[4,2,512,512]{2,3,1,0:T(8,128)} %get-tuple-element.67, f32[4,2,512]{2,1,0:T(2,128)S(1)} %get-tuple-element.66, bf16[4,512,2,64]{1,3,2,0:T(8,128)(2,1)S(1)} %bitcast.317, f32[4,512,2,1,64]{1,4,3,2,0:T(8,128)S(1)} %copy-done.9, ...), kind=kOutput, calls=%fused_computation.3 | convolution fusion | flops 275247104 | bytes 18384896 | tf_op jit(solution)/shard_map/tqhe,tkhe->thqk/dot_general | solution.py:664
  199.1 2.2 bitcast_reduce_fusion
  201.3 2.4 multiply_convert_fusion
  205.8 38.8 %all-reduce = (f32[2,4,768]{2,1,0:T(4,128)S(1)}, f32[6,1024]{1,0:T(8,128)S(1)}) all-reduce(f32[2,4,768]{2,1,0:T(4,128)S(1)} %pad_maximum_fusion.1, f32[6,1024]{1,0:T(8,128)S(1)} %stack.49), channel_id=1, replica_groups=mesh['fsdp'=4,'ctx'=2,'tp'=4] {'fsdp','ctx','tp'}, use_global_device_ids=true, to_apply=%region_14.15 | all-reduce | flops 12288 | bytes 98304 | tf_op jit(solution)/shard_map/psum | solution.py:762
  244.7 3.6 fusion.53
  248.6 3.8 fusion.50
  257.7 6.1 %pad_maximum_fusion = bf16[4,1024,1536]{1,2,0:T(8,128)(2,1)} fusion(bf16[4,1024,512]{1,2,0:T(8,128)(2,1)S(1)} %copy-done.5, bf16[4,1024,512]{1,2,0:T(8,128)(2,1)S(1)} %copy-done.4, bf16[4,1024,128]{1,2,0:T(8,128)(2,1)S(1)} %fusion.54, bf16[4,1024,384]{1,2,0:T(8,128)(2,1)S(1)} %convert_bitcast_fusion.2), kind=kLoop, calls=%fused_computation.1 | loop fusion | flops 50331648 | bytes 25165824 | tf_op jit(solution)/shard_map/concatenate | solution.py:767
  263.7 16.6 %copy.65 = bf16[4,1024,1536]{2,1,0:T(8,128)(2,1)} copy(bf16[4,1024,1536]{1,2,0:T(8,128)(2,1)} %pad_maximum_fusion) | data formatting | bytes 25165824 | tf_op jit(solution)/shard_map/concatenate | solution.py:767
  281.5 2.2 fusion.67.ig
  283.7 136.5 %scatter.1 = (f32[128,768]{1,0:T(8,128)}, f32[128,256]{1,0:T(8,128)}, f32[128,1024]{1,0:T(8,128)}, f32[128,1024]{1,0:T(8,128)}, bf16[2,2,64,1024]{3,2,1,0:T(8,128)(2,1)}, /*index=5*/bf16[2,2,64,1024]{3,2,1,0:T(8,128)(2,1)}) custom-call(bf16[4,2,2,2,128,1536]{5,4,3,2,1,0:T(8,128)(2,1)} %bitcast.253, bf16[256,1024]{1,0:T(8,128)(2,1)} %get-tuple-element.51.lo, ...), custom_call_target="tpu_custom_call" | custom-call | tf_op jit(solution)/shard_map/scatter/pallas_call | solution.py:632
  420.2 2.2 convert_element_type.188
  (161 shorter events, 45.4 us)
Async XLA Ops:
  0.6 7.2 %copy-start.20 = (bf16[512]{0:T(512)(128)(2,1)S(1)}, bf16[512]{0:T(512)(128)(2,1)}, u32[]{:S(2)}) copy-start(bf16[512]{0:T(512)(128)(2,1)} %param.15) | copy-start | bytes 3076
  0.7 7.2 %copy-start.19 = (bf16[1024]{0:T(1024)(128)(2,1)S(1)}, bf16[1024]{0:T(1024)(128)(2,1)}, u32[]{:S(2)}) copy-start(bf16[1024]{0:T(1024)(128)(2,1)} %param.18) | copy-start | bytes 6148
  0.7 127.1 %collective-permute-start = (s32[2,2,512]{2,1,0:T(2,128)}, s32[2,2,512]{2,1,0:T(2,128)S(1)}, u32[]{:S(2)}, u32[]{:S(2)}) collective-permute-start(s32[2,2,512]{2,1,0:T(2,128)} %param.13), channel_id=1, source_target_pairs={{0,8},{8,0},{16,24},{24,16},{1,9},{9,1},{17,25},{25,17},{2,10},{10... | collective-permute-start | bytes 24584 | tf_op jit(solution)/shard_map/ppermute | solution.py:651
  125.1 11.3 %copy-start.1 = (f32[4,384,512]{2,1,0:T(8,128)}, f32[4,384,512]{2,1,0:T(8,128)S(1)}, u32[]{:S(2)}) copy-start(f32[4,384,512]{2,1,0:T(8,128)S(1)} %fusion.34) | copy-start | bytes 9437188
  136.3 12.5 %slice-start.2 = ((s8[12582912]{0:T(1024)(128)(4,1)}), s8[4194304]{0:T(1024)(128)(4,1)S(1)}, s32[]{:S(2)}) async-start(s8[12582912]{0:T(1024)(128)(4,1)} %bitcast.279), calls=%async_computation.2 | async-start | bytes 8388608
  136.3 12.5 %slice-start.3 = ((s8[12582912]{0:T(1024)(128)(4,1)}), s8[4194304]{0:T(1024)(128)(4,1)S(1)}, s32[]{:S(2)}) async-start(s8[12582912]{0:T(1024)(128)(4,1)} %bitcast.279), calls=%async_computation.3 | async-start | bytes 8388608
  136.3 12.4 %slice-start.4 = ((s8[12582912]{0:T(1024)(128)(4,1)}), s8[4194304]{0:T(1024)(128)(4,1)S(1)}, s32[]{:S(2)}) async-start(s8[12582912]{0:T(1024)(128)(4,1)} %bitcast.279), calls=%async_computation.4 | async-start | bytes 8388608
  144.0 2.0 collective-permute-start.1
  146.8 13.0 %copy-start.10 = (bf16[256,1024]{1,0:T(8,128)(2,1)}, bf16[256,1024]{1,0:T(8,128)(2,1)S(1)}, u32[]{:S(2)}) copy-start(bf16[256,1024]{1,0:T(8,128)(2,1)S(1)} %fusion.79) | copy-start | bytes 1572868
  146.8 2.0 collective-permute-start.2
  148.8 11.1 %copy-start.21 = (bf16[256,1024]{1,0:T(8,128)(2,1)}, bf16[256,1024]{1,0:T(8,128)(2,1)S(1)}, u32[]{:S(2)}) copy-start(bf16[256,1024]{1,0:T(8,128)(2,1)S(1)} %collective-permute-done.2) | copy-start | bytes 1572868
  162.3 2.0 collective-permute-start.3
  167.0 6.1 %copy-start.13 = (bf16[256,1024]{1,0:T(8,128)(2,1)}, bf16[256,1024]{1,0:T(8,128)(2,1)S(1)}, u32[]{:S(2)}) copy-start(bf16[256,1024]{1,0:T(8,128)(2,1)S(1)} %get-tuple-element.53) | copy-start | bytes 1572868
  167.0 2.0 collective-permute-start.4
  177.6 2.1 collective-permute-start.5
  177.8 5.4 %copy-start.11 = (bf16[256,1024]{1,0:T(8,128)(2,1)S(1)}, bf16[256,1024]{1,0:T(8,128)(2,1)}, u32[]{:S(2)}) copy-start(bf16[256,1024]{1,0:T(8,128)(2,1)} %copy-done.10) | copy-start | bytes 1572868
  177.8 5.4 %copy-start.22 = (bf16[256,1024]{1,0:T(8,128)(2,1)S(1)}, bf16[256,1024]{1,0:T(8,128)(2,1)}, u32[]{:S(2)}) copy-start(bf16[256,1024]{1,0:T(8,128)(2,1)} %copy-done.21) | copy-start | bytes 1572868
  177.8 5.4 %copy-start.28 = (bf16[4,512,512]{2,1,0:T(8,128)(2,1)S(1)}, bf16[4,512,512]{2,1,0:T(8,128)(2,1)}, u32[]{:S(2)}) copy-start(bf16[4,512,512]{2,1,0:T(8,128)(2,1)} %copy-done.27) | copy-start | bytes 6291460
  183.0 8.9 %collective-permute-start.6 = (bf16[256,1024]{1,0:T(8,128)(2,1)}, bf16[256,1024]{1,0:T(8,128)(2,1)}, u32[]{:S(2)}, u32[]{:S(2)}) collective-permute-start(bf16[256,1024]{1,0:T(8,128)(2,1)} %get-tuple-element.55), channel_id=1, source_target_pairs={{0,8},{8,0},{16,24},{24,16},{1,9},{9,1},{17,25},{25,17},{2,10},{10... | collective-permute-start | bytes 1572872 | tf_op jit(solution)/shard_map/ppermute | solution.py:651
  191.9 7.1 %slice-start = ((s8[8388608]{0:T(1024)(128)(4,1)}), s8[4194304]{0:T(1024)(128)(4,1)S(1)}, s32[]{:S(2)}) async-start(s8[8388608]{0:T(1024)(128)(4,1)} %bitcast.254), calls=%async_computation | async-start | bytes 8388608
  203.7 40.9 %copy-start.3 = (f32[4,512,2,1,64]{1,4,3,2,0:T(8,128)S(1)}, f32[4,512,2,1,64]{1,4,3,2,0:T(8,128)}, u32[]{:S(2)}) copy-start(f32[4,512,2,1,64]{1,4,3,2,0:T(8,128)} %get-tuple-element.49) | copy-start | bytes 3145732
  252.5 5.1 %copy-start.5 = (bf16[4,1024,512]{1,2,0:T(8,128)(2,1)S(1)}, bf16[4,1024,512]{1,2,0:T(8,128)(2,1)}, u32[]{:S(2)}) copy-start(bf16[4,1024,512]{1,2,0:T(8,128)(2,1)} %convert_bitcast_fusion) | copy-start | bytes 12582916
  255.6 25.9 %collective-permute-start.7 = (bf16[256,1024]{1,0:T(8,128)(2,1)S(1)}, bf16[256,1024]{1,0:T(8,128)(2,1)S(1)}, u32[]{:S(2)}, u32[]{:S(2)}) collective-permute-start(bf16[256,1024]{1,0:T(8,128)(2,1)S(1)} %slice.227), channel_id=1, source_target_pairs={{0,8},{8,0},{16,24},{24,16},{1,9},{9,1},{17,25},{25,17},{2,10},{10... | collective-permute-start | bytes 1572872 | tf_op jit(solution)/shard_map/ppermute | solution.py:651
  420.2 9.3 %copy-start.12 = (f32[128,1024]{1,0:T(8,128)S(1)}, f32[128,1024]{1,0:T(8,128)}, u32[]{:S(2)}) copy-start(f32[128,1024]{1,0:T(8,128)} %get-tuple-element.100) | copy-start | bytes 1572868
  (18 other events, 59.6 us)

commit v2 on v1

--- a/solution.py
+++ b/solution.py
@@ -565,19 +565,21 @@
 
 PIECES = ((0, 384), (384, 128), (512, 512), (1024, 512))
 
-def scatter_kernel(g_in, lo, ig, o_qkv, o_out, o_up, o_down, lo_out, ig_out, g, ya, xa, xd, yd, adzr, adzl, bzr, bzl, by, bx, sib, send_sems, recv_sems, local_sems):
+def scatter_kernel(g_qkv, g_out, g_up, g_down, lo, ig, sums, o_qkv, o_out, o_up, o_down, lo_out, ig_out, sums_out, g, ya, xa, xd, yd, adzr, adzl, bzr, bzl, by, bx, sib, sums_run, sums_land, send_sems, recv_sems, local_sems):
     w = Where()
     sem, one, need = barrier(w)
     same = w.e == w.c
     for d in range(4):
         go = (lambda d=d: one(w.at(e=w.c, c=w.e, t=(w.t + d) % 4)))
         when(True if d else jnp.logical_not(same), go)
-    pl.semaphore_wait(sem, need + 3 + jnp.where(same, 0, 1))
+    one(w.at(t=(w.t + 2) % 4))
+    pl.semaphore_wait(sem, need + 4 + jnp.where(same, 0, 1))
     net = Net(send_sems, recv_sems)
     bufs = {"ya": ya, "xa": xa, "xd": xd, "yd": yd, "adzr": adzr, "adzl": adzl, "bzr": bzr, "bzl": bzl, "by": by, "bx": bx, "sib": sib}
     ranges = (1024, 512, 0)
-    copies = [pltpu.make_async_copy(g_in.at[..., pl.ds(c0, 512)], g.at[..., pl.ds(c0, 512)], local_sems.at[i]) for i, c0 in enumerate(ranges)]
-    for cp in copies:
+    copies = [[pltpu.make_async_copy(src, g.at[..., pl.ds(*PIECES[i])], local_sems.at[5 + i])] for src, i in ((g_down, 3), (g_up, 2), (g_qkv, 0))]
+    copies[2].append(pltpu.make_async_copy(g_out, g.at[..., pl.ds(*PIECES[1])], local_sems.at[6]))
+    for cp in sum(copies, []):
         cp.start()
     parts = [Scatter(net, w, g, bufs, c0, 512) for c0 in ranges]
     ids = [[net.pair(), net.pair()] for _ in range(4)]
@@ -594,6 +596,20 @@
         for d in range(4):
             t2 = (w.t + 4 - d) % 4
             net.recv(ids[d][k], True if d else jnp.logical_not(same), lambda t2=t2: dst.at[t2 // 2, t2 % 2], w.at(e=w.c, c=w.e, t=t2))
+    partners = (w.at(e=1 - w.e), w.at(c=1 - w.c), w.at(y=1 - w.y), w.at(t=w.t + 1 - 2 * (w.t % 2)), w.at(t=(w.t + 2) % 4))
+    sums_ids = [net.pair() for _ in partners]
+    def sums_step(s):
+        if s == 0:
+            sums_run[0] = sums[...]
+        else:
+            net.recv(sums_ids[s - 1], True, lambda: sums_land.at[s - 1], partners[s - 1])
+            total = sums_run[s - 1] + sums_land[s - 1]
+            if s == 5:
+                sums_out[...] = total
+            else:
+                sums_run[s] = total
+        if s < 5:
+            net.send(sums_ids[s], True, lambda: sums_run.at[s], lambda: sums_land.at[s], partners[s])
     own = []
     def finish(p):
         for (c0, cn), ref in zip(PIECES, (o_qkv, o_out, o_up, o_down)):
@@ -606,10 +622,13 @@
             k = s - start
             if 0 <= k <= 6:
                 if k == 0:
-                    copies[p].wait()
+                    for cp in copies[p]:
+                        cp.wait()
                 parts[p].stage(k)
                 if k == 6:
                     finish(p)
+        if s <= 5:
+            sums_step(s)
         if s == 0:
             own.append(rows_out(0, lo, lo_out, local_sems.at[3]))
         if s == 2:
@@ -620,31 +639,33 @@
     rows_in(1, ig_out)
     net.drain()
 
-N_SCATTER = 101
-
-def run_scatter(g, lo, ig):
+N_SCATTER = 106
+
+def run_scatter(grads, lo, ig, sums):
     any_ = pl.BlockSpec(memory_space=pl.ANY)
     vm = pl.BlockSpec(memory_space=pltpu.VMEM)
     f32, bf = jnp.float32, jnp.bfloat16
-    n = g.shape[-1]
+    grads = [a.reshape(4, 2, 2, 2, 128, -1) for a in grads]
+    n = sum(a.shape[-1] for a in grads)
     share = lo.shape[0] // 4
     sd = jax.ShapeDtypeStruct
     return pl.pallas_call(
         scatter_kernel,
         out_shape=(sd((128, 768), f32), sd((128, 256), f32), sd((128, 1024), f32), sd((128, 1024), f32),
-                   sd((2, 2, share, lo.shape[1]), lo.dtype), sd((2, 2, share, ig.shape[1]), ig.dtype)),
-        in_specs=[any_, vm, vm],
-        out_specs=(vm, vm, vm, vm, any_, any_),
-        scratch_shapes=[pltpu.VMEM(g.shape, bf),
+                   sd((2, 2, share, lo.shape[1]), lo.dtype), sd((2, 2, share, ig.shape[1]), ig.dtype), sd(sums.shape, f32)),
+        in_specs=[any_] * 4 + [vm] * 3,
+        out_specs=(vm, vm, vm, vm, any_, any_, vm),
+        scratch_shapes=[pltpu.VMEM((4, 2, 2, 2, 128, n), bf),
                         pltpu.VMEM((4, 2, 2, 48, n), bf), pltpu.VMEM((4, 2, 48, n), bf),
                         pltpu.VMEM((4, 2, 2, 48, n), bf), pltpu.VMEM((4, 2, 48, n), bf),
                         pltpu.VMEM((4, 2, 96, n), bf), pltpu.VMEM((4, 2, 96, n), bf),
                         pltpu.VMEM((4, 2, 2, 2, 32, n), bf), pltpu.VMEM((4, 2, 2, 2, 32, n), bf),
                         pltpu.VMEM((2, 2, 32, n), bf), pltpu.VMEM((2, 32, n), bf), pltpu.VMEM((128, n), bf),
-                        pltpu.SemaphoreType.DMA((N_SCATTER,)), pltpu.SemaphoreType.DMA((N_SCATTER,)), pltpu.SemaphoreType.DMA((5,))],
+                        pltpu.VMEM((5,) + sums.shape, f32), pltpu.VMEM((5,) + sums.shape, f32),
+                        pltpu.SemaphoreType.DMA((N_SCATTER,)), pltpu.SemaphoreType.DMA((N_SCATTER,)), pltpu.SemaphoreType.DMA((9,))],
         compiler_params=pltpu.CompilerParams(collective_id=1, has_side_effects=True),
         name="scatter",
-    )(g, lo, ig)
+    )(*grads, lo, ig, sums)
 
 
 def swap_cores(value):
@@ -759,17 +780,15 @@
     norm_sums = jnp.stack([gain_one, gain_two, shift_zero, shift_one, shift_two, shift_three])
     head_sums = jnp.concatenate([qv_grad.reshape(4, 256), up_bias_grad.reshape(4, 512)], axis=1)
     head_sums = jnp.stack([jnp.where(w.e == i, head_sums, 0.0) for i in range(2)])
-    norm_sums, head_sums = lax.psum((norm_sums, head_sums), ("fsdp", "ctx", "tp"))
+    sums = jnp.concatenate([norm_sums.reshape(48, 128), head_sums.reshape(48, 128)])
+    steps = [a.astype(bf) for a in (qkv_step, out_step, up_step, down_step)]
+    g_qkv, g_out, g_up, g_down, layer_out, input_out, sums = run_scatter(
+        steps, layer_mine, input_mine, sums
+    )
+    head_sums = sums[48:].reshape(2, 4, 768)
     head_mine = lax.dynamic_index_in_dim(head_sums, w.t, 1, keepdims=False)
     block = (2 * w.y + w.e) * 2 + w.c
-    norm_mine = lax.dynamic_slice_in_dim(norm_sums, block * 128, 128, 1)
-
-    steps = jnp.concatenate(
-        [a.astype(bf) for a in (qkv_step, out_step, up_step, down_step)], axis=-1
-    )
-    g_qkv, g_out, g_up, g_down, layer_out, input_out = run_scatter(
-        steps.reshape(4, 2, 2, 2, 128, -1), layer_mine, input_mine
-    )
+    norm_mine = lax.dynamic_index_in_dim(sums[:48].reshape(6, 8, 128), block, 1, keepdims=False)
     return (
         layer_out,
         input_out.astype(f32),

time: 436 us -> 396 us (0.908)
  blocking collectives: 38.8 us -> 0 us
  other arithmetic: 24.4 us -> 18.5 us
    psum x1 -> x0, blocking collectives: 38.8 us -> none  [fast_local(): lax.psum((norm_sums, head_sums), ('fsdp', 'ctx', 'tp'))]
    convert_element_type x0 -> x4, local copies, waits for them, and re-layouts: none -> 18.6 us  [fast_local(): steps = [a.astype(bf) for a in (qkv_step, out_step, up_step, down_step)]]
    concatenate x1 -> x0, local copies, waits for them, and re-layouts: 16.6 us -> none  [fast_local(): jnp.concatenate([a.astype(bf) for a in (qkv_step, out_step, up_step, down...]
    concatenate x1, other arithmetic: 6.06 us -> 0.62 us  [fast_local(): jnp.concatenate([norm_sums.reshape(48, 128), head_sums.reshape(48, 128)])]
    unnamed x84 -> x80, local copies, waits for them, and re-layouts: 16 us -> 15.5 us
  transfers between devices with their start and end apart: 8 -> 8, of which waited for: 5 -> 5; matrix products, arithmetic and copies ran while one was open for 12% -> 13% of each run, Pallas kernels for 26% -> 29%
where the time goes in v2:
time: 396 us; the launch traced here: 390 us
  Pallas kernels  248 us (63%)
  matrix products  71.2 us (18%)
  local copies, waits for them, and re-layouts  40.8 us (10%)
  other arithmetic  18.5 us (5%)
  waiting for transfers between devices  7.75 us (2%)
    pallas_call x1, Pallas kernels, run_scatter(): pl.pallas_call(scatter_kernel, out_shape=(sd((128, 768), f32), sd((128, 2...  136 us
    pallas_call x1, Pallas kernels, run_gather(): pl.pallas_call(gather_kernel, out_shape=(jax.ShapeDtypeStruct((4, 2, 2, 2...  112 us
    dot_general x17, matrix products, dot32(): return jnp.einsum(spec, left, right, preferred_element_type=jnp.float32)  63.5 us
    convert_element_type x4, local copies, waits for them, and re-layouts, fast_local(): steps = [a.astype(bf) for a in (qkv_step, out_step, up_step, down_step)]  18.6 us
    unnamed x80, local copies, waits for them, and re-layouts  15.5 us
  transfers between devices with their start and end apart: 8, of which 5 were waited for; matrix products, arithmetic and copies ran while one was open for 13% of the time, Pallas kernels for 29%

profile of v2, /device:TPU:0, one launch (start us, length us, event | category | flops | bytes accessed | tf_op | source)
XLA Modules:
  0.0 390.3 jit_solution(10531052347492737892)
XLA Ops:
  8.5 112.5 %gather.1 = (bf16[4,2,2,2,128,1536]{5,4,3,2,1,0:T(8,128)(2,1)}, bf16[4,2,2,2,16,128]{5,4,3,2,1,0:T(8,128)(2,1)}, bf16[2,256,1024]{2,1,0:T(8,128)(2,1)}, bf16[256,1024]{1,0:T(8,128)(2,1)}) custom-call(bf16[2,128,1536]{2,1,0:T(8,128)(2,1)} %maximum_bitcast_fusion.3.mine, bf16[2,16,128]{2,1,0:T(8,128)(2,1)} %maximum_maximum_fusion.small, ...), custom_call_target="tpu_custom_call" | custom-call | tf_op jit(solution)/shard_map/gather/pallas_call | solution.py:482
  121.0 4.0 %fusion.34 = f32[4,384,512]{2,1,0:T(8,128)S(1)} fusion(bf16[512,1024,1]{1,0,2:T(8,128)(2,1)} %bitcast.283, bf16[4,1024,1536]{2,1,0:T(8,128)(2,1)} %bitcast.289), kind=kOutput, calls=%fused_computation.52 | convolution fusion | flops 1610612736 | bytes 7340032 | tf_op jit(solution)/shard_map/nk,tkc->tnc/dot_general | solution.py:685
  125.1 1.9 fusion.109
  128.7 7.7 %fusion.112 = (f32[4,2,512]{2,1,0:T(2,128)S(1)}, f32[4,2,512,512]{2,3,1,0:T(8,128)}) fusion(pred[512,512]{0,1:T(8,128)(4,1)S(1)} %broadcast_compare_fusion, f32[4,512,2,1,64]{1,4,3,2,0:T(8,128)} %get-tuple-element.49, f32[4,2,64]{2,1,0:T(2,128)S(1)} %bitcast.315, f32[4,512,2,3,64]{1,4,3,2,0:T(8,128)S(1)} %bitcast.270), kind=kOutput, calls=%fused_computation.175 | convolution fusion | flops 277348864 | bytes 10244096 | tf_op jit(solution)/shard_map/sub | solution.py:735
  136.4 4.7 %fusion.55 = bf16[4,2,64,512]{3,2,1,0:T(8,128)(2,1)S(1)} fusion(f32[4,512,2,1,64]{1,4,3,2,0:T(8,128)} %get-tuple-element.50, f32[4,2,64]{2,1,0:T(2,128)S(1)} %bitcast.322, f32[4,2,512,512]{2,3,1,0:T(8,128)} %get-tuple-element.69, f32[4,2,512]{2,1,0:T(2,128)S(1)} %get-tuple-element.68), kind=kOutput, calls=%fused_computation.74 | convolution fusion | flops 273416192 | bytes 9979904 | tf_op jit(solution)/shard_map/thqk,tkhe->tqhe/dot_general | solution.py:685
  141.2 2.8 convolution_bitcast_fusion
  148.9 11.0 %fusion.10 = (bf16[4,512,512]{2,1,0:T(8,128)(2,1)S(1)}, f32[4,512,512]{2,1,0:T(8,128)S(1)}, f32[4,512,512]{1,2,0:T(8,128)S(1)}) fusion(f32[4,512]{1,0:T(4,128)S(1)} %bitcast.319, bf16[4,1024,1536]{2,1,0:T(8,128)(2,1)S(1)} %bitcast.295, bf16[256,1024]{1,0:T(8,128)(2,1)S(1)} %collective-permute-done.2, bf16[256,1024]{1,0:T(8,128)(2,1)S(1)} %fusion.79), kind=kOutput, calls=%fused_computation.22 | convolution fusion | flops 2218786816 | bytes 15736832 | tf_op jit(solution)/shard_map/nk,tkc->tnc/dot_general | solution.py:685
  160.0 2.4 fusion.47
  169.1 4.1 %fusion.117 = (f32[4,512]{1,0:T(4,128)S(1)}, bf16[4,512,512]{2,1,0:T(8,128)(2,1)S(1)}) fusion(f32[4,512,512]{2,1,0:T(8,128)S(1)} %get-tuple-element.46, bf16[4,1024,1536]{2,1,0:T(8,128)(2,1)S(1)} %bitcast.297, bf16[256,1024]{1,0:T(8,128)(2,1)S(1)} %collective-permute-done.4, bf16[256,1024]{1,0:T(8,128)(2,1)S(1)} %get-tuple-element.53, ...), kind=kOutput, calls=%fused_computation.176 | convolution fusion | flops 2166355968 | bytes 15745024 | tf_op jit(solution)/shard_map/nk,tkc->tnc/dot_general | solution.py:685
  173.2 2.4 fusion.44
  177.9 2.0 collective-permute-done.5
  182.5 4.3 %convert_bitcast_fusion = bf16[4,1024,512]{1,2,0:T(8,128)(2,1)} fusion(bf16[4,512,512]{2,1,0:T(8,128)(2,1)S(1)} %copy-done.25, bf16[256,1024]{1,0:T(8,128)(2,1)S(1)} %copy-done.23, bf16[256,1024]{1,0:T(8,128)(2,1)S(1)} %copy-done.13), kind=kOutput, calls=%fused_computation.23 | convolution fusion | flops 2151677952 | bytes 7340032 | tf_op jit(solution)/shard_map/nk,tnc->tkc/dot_general | solution.py:685
  186.8 6.3 %copy.72 = bf16[4,1024,512]{2,1,0:T(8,128)(2,1)} copy(bf16[4,1024,512]{1,2,0:T(8,128)(2,1)} %convert_bitcast_fusion) | data formatting | bytes 8388608 | tf_op jit(solution)/shard_map/convert_element_type | solution.py:784
  193.2 5.9 %convert_bitcast_fusion.1 = bf16[4,1024,512]{1,2,0:T(8,128)(2,1)} fusion(bf16[4,512,512]{2,1,0:T(8,128)(2,1)} %copy-done.26, bf16[256,1024]{1,0:T(8,128)(2,1)S(1)} %copy-done.21, bf16[256,1024]{1,0:T(8,128)(2,1)S(1)} %copy-done.9), kind=kOutput, calls=%fused_computation.24 | convolution fusion | flops 2151677952 | bytes 7340032 | tf_op jit(solution)/shard_map/nk,tnc->tkc/dot_general | solution.py:685
  199.1 6.2 %copy.70 = bf16[4,1024,512]{2,1,0:T(8,128)(2,1)} copy(bf16[4,1024,512]{1,2,0:T(8,128)(2,1)} %convert_bitcast_fusion.1) | data formatting | bytes 8388608 | tf_op jit(solution)/shard_map/convert_element_type | solution.py:784
  205.4 2.3 convolution_convert_fusion.1
  207.7 4.6 %multiply_reduce_fusion = (f32[4,2,512]{2,1,0:T(2,128)S(1)}, f32[4,2,512,512]{2,3,1,0:T(8,128)S(1)}) fusion(f32[4,2,512,512]{2,3,1,0:T(8,128)} %get-tuple-element.69, f32[4,2,512]{2,1,0:T(2,128)S(1)} %get-tuple-element.68, bf16[4,512,2,64]{1,3,2,0:T(8,128)(2,1)S(1)} %bitcast.333, f32[4,512,2,1,64]{1,4,3,2,0:T(8,128)S(1)} %copy-done.7, ...), kind=kOutput, calls=%fused_computation.2 | convolution fusion | flops 275247104 | bytes 18384896 | tf_op jit(solution)/shard_map/tqhe,tkhe->thqk/dot_general | solution.py:685
  214.0 2.6 multiply_convert_fusion
  219.8 4.3 %fusion.50 = f32[512,1024]{1,0:T(8,128)S(1)} fusion(bf16[4,512,384]{1,2,0:T(8,128)(2,1)S(1)} %bitcast.274, bf16[4,1024,1536]{2,1,0:T(8,128)(2,1)} %bitcast.292), kind=kOutput, calls=%fused_computation.63 | convolution fusion | flops 1610612736 | bytes 6815744 | tf_op jit(solution)/shard_map/tnc,tkc->nk/dot_general | solution.py:685
  229.0 5.1 %convert_bitcast_fusion.2 = bf16[4,1024,384]{1,2,0:T(8,128)(2,1)} fusion(bf16[4,512,384]{1,2,0:T(8,128)(2,1)} %bitcast.275, bf16[512,1024,1]{1,0,2:T(8,128)(2,1)} %bitcast.284), kind=kOutput, calls=%fused_computation.51 | convolution fusion | flops 1612185600 | bytes 5767168 | tf_op jit(solution)/shard_map/nk,tnc->tkc/dot_general | solution.py:685
  234.1 4.7 %copy.67 = bf16[4,1024,384]{2,1,0:T(8,128)(2,1)} copy(bf16[4,1024,384]{1,2,0:T(8,128)(2,1)} %convert_bitcast_fusion.2) | data formatting | bytes 6291456 | tf_op jit(solution)/shard_map/convert_element_type | solution.py:784
  239.4 2.3 fusion.67.ig
  241.8 135.8 %scatter.1 = (f32[128,768]{1,0:T(8,128)}, f32[128,256]{1,0:T(8,128)}, f32[128,1024]{1,0:T(8,128)}, f32[128,1024]{1,0:T(8,128)}, bf16[2,2,64,1024]{3,2,1,0:T(8,12...) custom-call(bf16[4,2,2,2,128,384]{5,4,3,2,1,0:T(8,128)(2,1)} %bitcast.266, ...), custom_call_target="tpu_custom_call" | custom-call | tf_op jit(solution)/shard_map/scatter/pallas_call | solution.py:652
  378.6 2.1 convert_element_type.188
  (162 shorter events, 46.2 us)
Async XLA Ops:
  0.6 7.2 %copy-start.19 = (bf16[512]{0:T(512)(128)(2,1)S(1)}, bf16[512]{0:T(512)(128)(2,1)}, u32[]{:S(2)}) copy-start(bf16[512]{0:T(512)(128)(2,1)} %param.15) | copy-start | bytes 3076
  0.7 7.2 %copy-start.18 = (bf16[1024]{0:T(1024)(128)(2,1)S(1)}, bf16[1024]{0:T(1024)(128)(2,1)}, u32[]{:S(2)}) copy-start(bf16[1024]{0:T(1024)(128)(2,1)} %param.18) | copy-start | bytes 6148
  0.7 127.1 %collective-permute-start = (s32[2,2,512]{2,1,0:T(2,128)}, s32[2,2,512]{2,1,0:T(2,128)S(1)}, u32[]{:S(2)}, u32[]{:S(2)}) collective-permute-start(s32[2,2,512]{2,1,0:T(2,128)} %param.13), channel_id=1, source_target_pairs={{0,8},{8,0},{16,24},{24,16},{1,9},{9,1},{17,25},{25,17},{2,10},{10... | collective-permute-start | bytes 24584 | tf_op jit(solution)/shard_map/ppermute | solution.py:672
  125.1 11.4 %copy-start = (f32[4,384,512]{2,1,0:T(8,128)}, f32[4,384,512]{2,1,0:T(8,128)S(1)}, u32[]{:S(2)}) copy-start(f32[4,384,512]{2,1,0:T(8,128)S(1)} %fusion.34) | copy-start | bytes 9437188
  136.4 12.5 %slice-start.2 = ((s8[12582912]{0:T(1024)(128)(4,1)}), s8[4194304]{0:T(1024)(128)(4,1)S(1)}, s32[]{:S(2)}) async-start(s8[12582912]{0:T(1024)(128)(4,1)} %bitcast.293), calls=%async_computation.2 | async-start | bytes 8388608
  136.4 12.5 %slice-start.3 = ((s8[12582912]{0:T(1024)(128)(4,1)}), s8[4194304]{0:T(1024)(128)(4,1)S(1)}, s32[]{:S(2)}) async-start(s8[12582912]{0:T(1024)(128)(4,1)} %bitcast.293), calls=%async_computation.3 | async-start | bytes 8388608
  136.4 12.5 %slice-start.4 = ((s8[12582912]{0:T(1024)(128)(4,1)}), s8[4194304]{0:T(1024)(128)(4,1)S(1)}, s32[]{:S(2)}) async-start(s8[12582912]{0:T(1024)(128)(4,1)} %bitcast.293), calls=%async_computation.4 | async-start | bytes 8388608
  144.1 2.0 collective-permute-start.1
  146.9 13.1 %copy-start.8 = (bf16[256,1024]{1,0:T(8,128)(2,1)}, bf16[256,1024]{1,0:T(8,128)(2,1)S(1)}, u32[]{:S(2)}) copy-start(bf16[256,1024]{1,0:T(8,128)(2,1)S(1)} %fusion.79) | copy-start | bytes 1572868
  146.9 2.0 collective-permute-start.2
  148.9 11.1 %copy-start.20 = (bf16[256,1024]{1,0:T(8,128)(2,1)}, bf16[256,1024]{1,0:T(8,128)(2,1)S(1)}, u32[]{:S(2)}) copy-start(bf16[256,1024]{1,0:T(8,128)(2,1)S(1)} %collective-permute-done.2) | copy-start | bytes 1572868
  162.4 2.0 collective-permute-start.3
  167.1 6.1 %copy-start.12 = (bf16[256,1024]{1,0:T(8,128)(2,1)}, bf16[256,1024]{1,0:T(8,128)(2,1)S(1)}, u32[]{:S(2)}) copy-start(bf16[256,1024]{1,0:T(8,128)(2,1)S(1)} %get-tuple-element.53) | copy-start | bytes 1572868
  167.1 2.0 collective-permute-start.4
  177.7 2.1 collective-permute-start.5
  182.3 23.1 %copy-start.14 = (bf16[256,1024]{1,0:T(8,128)(2,1)}, bf16[256,1024]{1,0:T(8,128)(2,1)S(1)}, u32[]{:S(2)}) copy-start(bf16[256,1024]{1,0:T(8,128)(2,1)S(1)} %get-tuple-element.55) | copy-start | bytes 1572868
  182.3 23.1 %collective-permute-start.6 = (bf16[256,1024]{1,0:T(8,128)(2,1)S(1)}, bf16[256,1024]{1,0:T(8,128)(2,1)}, u32[]{:S(2)}, u32[]{:S(2)}) collective-permute-start(bf16[256,1024]{1,0:T(8,128)(2,1)S(1)} %get-tuple-element.55), channel_id=1, source_target_pairs={{0,8},{8,0},{16,24},{24,16},{1,9},{9,1},{17,25},{25,17},{2,10},{10... | collective-permute-start | bytes 1572872 | tf_op jit(solution)/shard_map/ppermute | solution.py:672
  186.8 6.3 %copy-start.9 = (bf16[256,1024]{1,0:T(8,128)(2,1)S(1)}, bf16[256,1024]{1,0:T(8,128)(2,1)}, u32[]{:S(2)}) copy-start(bf16[256,1024]{1,0:T(8,128)(2,1)} %copy-done.8) | copy-start | bytes 1572868
  186.8 6.3 %copy-start.21 = (bf16[256,1024]{1,0:T(8,128)(2,1)S(1)}, bf16[256,1024]{1,0:T(8,128)(2,1)}, u32[]{:S(2)}) copy-start(bf16[256,1024]{1,0:T(8,128)(2,1)} %copy-done.20) | copy-start | bytes 1572868
  205.4 6.9 %slice-start = ((s8[8388608]{0:T(1024)(128)(4,1)}), s8[4194304]{0:T(1024)(128)(4,1)S(1)}, s32[]{:S(2)}) async-start(s8[8388608]{0:T(1024)(128)(4,1)} %bitcast.267), calls=%async_computation | async-start | bytes 8388608
  219.8 6.1 %copy-start.15 = (bf16[256,1024]{1,0:T(8,128)(2,1)S(1)}, bf16[256,1024]{1,0:T(8,128)(2,1)}, u32[]{:S(2)}) copy-start(bf16[256,1024]{1,0:T(8,128)(2,1)} %copy-done.14) | copy-start | bytes 1572868
  225.5 13.9 %collective-permute-start.7 = (bf16[256,1024]{1,0:T(8,128)(2,1)S(1)}, bf16[256,1024]{1,0:T(8,128)(2,1)}, u32[]{:S(2)}, u32[]{:S(2)}) collective-permute-start(bf16[256,1024]{1,0:T(8,128)(2,1)S(1)} %slice.242), channel_id=1, source_target_pairs={{0,8},{8,0},{16,24},{24,16},{1,9},{9,1},{17,25},{25,17},{2,10},{10... | collective-permute-start | bytes 1572872 | tf_op jit(solution)/shard_map/ppermute | solution.py:672
  377.6 10.6 %copy-start.11 = (f32[128,1024]{1,0:T(8,128)S(1)}, f32[128,1024]{1,0:T(8,128)}, u32[]{:S(2)}) copy-start(f32[128,1024]{1,0:T(8,128)} %get-tuple-element.100) | copy-start | bytes 1572868
  377.6 11.4 %copy-start.10 = (f32[128,1024]{1,0:T(8,128)S(1)}, f32[128,1024]{1,0:T(8,128)}, u32[]{:S(2)}) copy-start(f32[128,1024]{1,0:T(8,128)} %get-tuple-element.102) | copy-start | bytes 1572868
  (16 other events, 51.3 us)
